TPU v7x, 128 devices: a whole 4x4x4 slice. The times are simulated.
128 devices in a mesh: ctx: 32 (over x, z, core), head: 4 (over y).
Axes of the slice: x: 4, y: 4, z: 4, core: 2. Of those that a mesh axis runs over, the one named last changes fastest.
Arguments:
- query_proj: bfloat16 [4096, 4096], P('ctx', 'head'), may hold values from -4 to 4
- key_proj: bfloat16 [4096, 4096], P('ctx', 'head'), may hold values from -6 to 6
- value_proj: bfloat16 [4096, 4096], P('ctx', 'head'), may hold values from -6 to 6
- grad_out: bfloat16 [4096, 4096], P('ctx', 'head'), may hold values from -4 to 4
- out_proj: bfloat16 [4096, 4096], P('head'), may hold values from -0.09375 to 0.09375
- filters: bfloat16 [256, 4096], P('head'), may hold values from -1 to 1, as said below
- skip_gain: float32 [4096], P('head'), may hold values from 0.5 to 1.5
- doc_lengths: int32 [4], replicated, may hold values from 1 to 17, 32 in all
- group_of: int32 [4096], P('head'), may hold values from 0 to 255, as said below
Outputs:
- grad_query: bfloat16 [4096, 4096], P('ctx', 'head')
- grad_key: bfloat16 [4096, 4096], P('ctx', 'head')
- grad_filters: float32 [256, 4096], P('head', 'ctx')
Inputs may be any that keep to these rules, and one draw needn't show every extreme that they name: `filters`: filter entries never above 1 in magnitude. `group_of`: each filter group is named by exactly 16 channels, and the channels of the k-th block of 1024 channels name only groups k * 64 to (k + 1) * 64 - 1.
All inputs are finite; a program needn't handle non-finite values.
Results may differ from a plain program's by a relative error of at most 0.005.
Values may be sent and summed in bfloat16 or wider, within the bound.
A program may use at most 128 MiB of HBM per device.

v0:
```python
import jax
import jax.numpy as jnp
from jax import lax
from jax.sharding import PartitionSpec as P


def skew_rows(vector, block_rows):
    lead = vector.shape[:-1]
    extended = jnp.concatenate([vector, jnp.zeros(lead + (1,), vector.dtype)], -1)
    tiled = jnp.broadcast_to(extended[..., None, :], lead + (block_rows, 2 * block_rows + 1))
    tiled = tiled.reshape(lead + (block_rows * (2 * block_rows + 1),))
    shaped = tiled[..., : 2 * block_rows * block_rows].reshape(lead + (block_rows, 2 * block_rows))
    return shaped[..., block_rows:]


def diagonal_sums(matrix, block_rows):
    lead = matrix.shape[:-2]
    padded = jnp.concatenate([jnp.zeros(lead + (block_rows, block_rows), matrix.dtype), matrix], -1)
    flat = padded.reshape(lead + (2 * block_rows * block_rows,))
    flat = jnp.concatenate([flat, jnp.zeros(lead + (block_rows,), matrix.dtype)], -1)
    rows_view = flat.reshape(lead + (block_rows, 2 * block_rows + 1))
    return jnp.sum(rows_view[..., : 2 * block_rows], axis=-2)


def span_documents(doc_lengths, count):
    bounds = jnp.cumsum(doc_lengths)
    positions = jnp.arange(count, dtype=jnp.int32)
    return jnp.sum((bounds[None, :] <= positions[:, None]).astype(jnp.int32), axis=1)


def keep_state(state):
    return state


def per_device(
    query_proj, key_proj, value_proj, grad_out, out_proj, filters, skip_gain, doc_lengths, group_of
):
    block_rows = query_proj.shape[0]
    channels = query_proj.shape[1]
    groups_here = filters.shape[0]
    per_group = channels // groups_here
    spans = lax.axis_size("ctx")
    position = lax.axis_index("ctx")
    feature_grad = jnp.einsum(
        "tm,cm->tc",
        lax.all_gather(grad_out, "head", axis=1, tiled=True),
        out_proj,
        preferred_element_type=jnp.float32,
    )
    conv_grad = (feature_grad * value_proj.astype(jnp.float32)).astype(jnp.bfloat16)
    local_group = group_of - lax.axis_index("head") * groups_here
    ranking = jnp.argsort(local_group)
    inverse = jnp.argsort(ranking)
    grad_sorted = jnp.take(conv_grad, ranking, axis=1)
    query_sorted = jnp.take(query_proj, ranking, axis=1)
    key_sorted = jnp.take(key_proj, ranking, axis=1)
    skip_sorted = jnp.take(skip_gain, ranking)
    span_doc = span_documents(doc_lengths, spans)
    zero_rim = jnp.zeros((groups_here, block_rows), filters.dtype)
    filt_padded = jnp.concatenate([zero_rim, filters, zero_rim], 1)
    gated = (query_sorted.astype(jnp.float32) * key_sorted.astype(jnp.float32)).astype(jnp.bfloat16)
    own_grad = grad_sorted.reshape(block_rows, groups_here, per_group)
    own_doc = span_doc[position]
    start_state = (
        jnp.zeros((block_rows, groups_here, per_group), jnp.float32),
        jnp.zeros((groups_here, block_rows * (spans + 2)), jnp.float32),
    )
    carry = start_state
    grad_piece = lax.all_gather(grad_sorted, "ctx", axis=0, tiled=True)
    gate_piece = lax.all_gather(gated, "ctx", axis=0, tiled=True)
    count = grad_piece.shape[0] // block_rows
    grad_pieces = grad_piece.reshape(count, block_rows, groups_here, per_group)
    gate_pieces = gate_piece.reshape(count, block_rows, groups_here, per_group)

    def step(state_in, entry):
        grad_block, gate_block, offset = entry
        same = span_doc[jnp.clip(offset, 0, spans - 1)] == own_doc
        ahead = offset - position
        behind = position - offset

        def later_work(state):
            grad_acc, lag_acc = state
            window = lax.dynamic_slice_in_dim(filt_padded, ahead * block_rows, 2 * block_rows, 1)
            toeplitz = skew_rows(window, block_rows)
            grad_acc = grad_acc + jnp.einsum(
                "gst,tgc->sgc", toeplitz, grad_block, preferred_element_type=jnp.float32
            )
            return (grad_acc, lag_acc)

        def earlier_work(state):
            grad_acc, lag_acc = state
            corr = jnp.einsum(
                "sgc,tgc->gst", gate_block, own_grad, preferred_element_type=jnp.float32
            )
            sums = diagonal_sums(corr, block_rows)
            before = lax.dynamic_slice_in_dim(lag_acc, behind * block_rows, 2 * block_rows, 1)
            lag_acc = lax.dynamic_update_slice_in_dim(
                lag_acc, before + sums, behind * block_rows, 1
            )
            return (grad_acc, lag_acc)

        state_mid = lax.cond(same & (ahead >= 0), later_work, keep_state, state_in)
        state_out = lax.cond(same & (behind >= 0), earlier_work, keep_state, state_mid)
        return (state_out, None)

    carry, _ = lax.scan(step, carry, (grad_pieces, gate_pieces, jnp.arange(count, dtype=jnp.int32)))
    gated_grad, lag_padded = carry
    gated_grad = gated_grad.reshape(block_rows, channels) + skip_sorted[
        None, :
    ] * grad_sorted.astype(jnp.float32)
    query_out = (gated_grad * key_sorted.astype(jnp.float32)).astype(jnp.bfloat16)
    key_out = (gated_grad * query_sorted.astype(jnp.float32)).astype(jnp.bfloat16)
    lag_terms = lag_padded[:, block_rows : block_rows + block_rows * spans]
    grad_filters = lax.psum_scatter(lag_terms, "ctx", scatter_dimension=1, tiled=True)
    grad_query = jnp.take(query_out, inverse, axis=1)
    grad_key = jnp.take(key_out, inverse, axis=1)
    return (grad_query, grad_key, grad_filters)


def solution(mesh):
    in_specs = (
        P("ctx", "head"),
        P("ctx", "head"),
        P("ctx", "head"),
        P("ctx", "head"),
        P("head", None),
        P("head", None),
        P("head"),
        P(),
        P("head"),
    )
    out_specs = (P("ctx", "head"), P("ctx", "head"), P("head", "ctx"))
    return jax.shard_map(
        per_device, mesh=mesh, in_specs=in_specs, out_specs=out_specs, check_vma=False
    )
```

profile of v0, /device:TPU:1, one launch (start us, length us, event | category | flops | bytes accessed | tf_op | source)
XLA Modules:
  0.0 935.6 jit_solution(11843048497270120990)
XLA Ops:
  48.5 51.6 %all-gather.8.cloned.1.call-done = bf16[4096,1024]{0,1:T(8,128)(2,1)} async-done(((bf16[128,1024]{0,1:T(8,128)(2,1)}), bf16[4096,1024]{0,1:T(8,128)(2,1)}) %all-gather.8.cloned.1.call-update) | async-done | bytes 8388624 | tf_op jit(solution)/shard_map/all_gather | solution.py:70
  119.7 42.4 %all-gather.6.cloned.1.call-done = bf16[4096,1024]{0,1:T(8,128)(2,1)} async-done(((bf16[128,1024]{0,1:T(8,128)(2,1)}), bf16[4096,1024]{0,1:T(8,128)(2,1)}) %all-gather.6.cloned.1.call-update) | async-done | bytes 8388624 | tf_op jit(solution)/shard_map/all_gather | solution.py:69
  181.8 518.8 %while.18 = (s32[]{:T(128)}, f32[128,64,16]{0,2,1:T(8,128)S(1)}, f32[64,4352]{1,0:T(8,128)S(1)}, s32[32]{0:T(128)S(1)}, s32[32]{0:T(128)S(1)}, /*index=5*/s32[]{...) while((s32[]{:T(128)}, f32[128,64,16]{0,2,1:T(8,128)S(1)}, ...), condition=%wide.region_9.11_spmd, body=%wide.region_3.10_spmd.sunk | while | flops 69337104 | bytes 113559256 | solution.py:106
  186.5 29.8 %conditional.5 = (f32[64,4352]{1,0:T(8,128)S(1)}) conditional(s32[]{:T(128)} %convert_element_type.70, f32[64,4352]{1,0:T(8,128)S(1)} %get-tuple-element.285, (s32[]{:T(128)}, f32[64,4352]{1,0:T(8,128)S(1)}, bf16[32,128,64,16]{1,3,2,0:T(8,128)(2,1)}, s32[]{:T(128)}, bf16[128,64,16]{0,2,1:T(8,128)(2,1)S(1)}) %tuple.51), branch_computations={%region_6.7_spmd, %region_7.9_spmd} | conditional | flops 35651588 | bytes 76382776 | solution.py:103
  197.8 14.2 %reshape.66 = f32[64,128,257]{2,1,0:T(8,128)} reshape(f32[64,32896]{1,0:T(8,128)} %concatenate.10) | data formatting | bytes 16842752 | tf_op jit(solution)/shard_map/while/body/eval_jaxpr/cond/branch_1_fun/reshape | solution.py:21
  220.3 19.5 %conditional.4 = (f32[128,64,16]{0,2,1:T(8,128)S(1)}) conditional(s32[]{:T(128)} %convert_element_type.69, f32[128,64,16]{0,2,1:T(8,128)S(1)} %get-tuple-element.284, (s32[]{:T(128)}, bf16[64,4352]{1,0:T(8,128)(2,1)S(1)}, bf16[32,128,64,16]{1,3,2,0:T(8,128)(2,1)}, s32[]{:T(128)}, f32[128,64,16]{0,2,1:T(8,128)S(1)}) %tuple.50), branch_computations={%region_4.5_spmd, %region_5.6_spmd} | conditional | flops 33685508 | bytes 37176148 | solution.py:102
  223.5 10.9 %reshape.63 = bf16[64,32896]{1,0:T(8,128)(2,1)} reshape(bf16[64,128,257]{2,1,0:T(8,128)(2,1)} %broadcast_in_dim.30) | data formatting | bytes 8421376 | tf_op jit(solution)/shard_map/while/body/eval_jaxpr/cond/branch_1_fun/reshape | solution.py:11
  240.5 29.8 %conditional.5 = (f32[64,4352]{1,0:T(8,128)S(1)}) conditional(s32[]{:T(128)} %convert_element_type.70, f32[64,4352]{1,0:T(8,128)S(1)} %get-tuple-element.285, (s32[]{:T(128)}, f32[64,4352]{1,0:T(8,128)S(1)}, bf16[32,128,64,16]{1,3,2,0:T(8,128)(2,1)}, s32[]{:T(128)}, bf16[128,64,16]{0,2,1:T(8,128)(2,1)S(1)}) %tuple.51), branch_computations={%region_6.7_spmd, %region_7.9_spmd} | conditional | flops 35651588 | bytes 76382776 | solution.py:103
  251.8 14.2 %reshape.66 = f32[64,128,257]{2,1,0:T(8,128)} reshape(f32[64,32896]{1,0:T(8,128)} %concatenate.10) | data formatting | bytes 16842752 | tf_op jit(solution)/shard_map/while/body/eval_jaxpr/cond/branch_1_fun/reshape | solution.py:21
  274.2 19.5 %conditional.4 = (f32[128,64,16]{0,2,1:T(8,128)S(1)}) conditional(s32[]{:T(128)} %convert_element_type.69, f32[128,64,16]{0,2,1:T(8,128)S(1)} %get-tuple-element.284, (s32[]{:T(128)}, bf16[64,4352]{1,0:T(8,128)(2,1)S(1)}, bf16[32,128,64,16]{1,3,2,0:T(8,128)(2,1)}, s32[]{:T(128)}, f32[128,64,16]{0,2,1:T(8,128)S(1)}) %tuple.50), branch_computations={%region_4.5_spmd, %region_5.6_spmd} | conditional | flops 33685508 | bytes 37176148 | solution.py:102
  277.4 10.9 %reshape.63 = bf16[64,32896]{1,0:T(8,128)(2,1)} reshape(bf16[64,128,257]{2,1,0:T(8,128)(2,1)} %broadcast_in_dim.30) | data formatting | bytes 8421376 | tf_op jit(solution)/shard_map/while/body/eval_jaxpr/cond/branch_1_fun/reshape | solution.py:11
  298.3 19.5 %conditional.4 = (f32[128,64,16]{0,2,1:T(8,128)S(1)}) conditional(s32[]{:T(128)} %convert_element_type.69, f32[128,64,16]{0,2,1:T(8,128)S(1)} %get-tuple-element.284, (s32[]{:T(128)}, bf16[64,4352]{1,0:T(8,128)(2,1)S(1)}, bf16[32,128,64,16]{1,3,2,0:T(8,128)(2,1)}, s32[]{:T(128)}, f32[128,64,16]{0,2,1:T(8,128)S(1)}) %tuple.50), branch_computations={%region_4.5_spmd, %region_5.6_spmd} | conditional | flops 33685508 | bytes 37176148 | solution.py:102
  301.6 10.9 %reshape.63 = bf16[64,32896]{1,0:T(8,128)(2,1)} reshape(bf16[64,128,257]{2,1,0:T(8,128)(2,1)} %broadcast_in_dim.30) | data formatting | bytes 8421376 | tf_op jit(solution)/shard_map/while/body/eval_jaxpr/cond/branch_1_fun/reshape | solution.py:11
  322.4 19.5 %conditional.4 = (f32[128,64,16]{0,2,1:T(8,128)S(1)}) conditional(s32[]{:T(128)} %convert_element_type.69, f32[128,64,16]{0,2,1:T(8,128)S(1)} %get-tuple-element.284, (s32[]{:T(128)}, bf16[64,4352]{1,0:T(8,128)(2,1)S(1)}, bf16[32,128,64,16]{1,3,2,0:T(8,128)(2,1)}, s32[]{:T(128)}, f32[128,64,16]{0,2,1:T(8,128)S(1)}) %tuple.50), branch_computations={%region_4.5_spmd, %region_5.6_spmd} | conditional | flops 33685508 | bytes 37176148 | solution.py:102
  325.7 10.9 %reshape.63 = bf16[64,32896]{1,0:T(8,128)(2,1)} reshape(bf16[64,128,257]{2,1,0:T(8,128)(2,1)} %broadcast_in_dim.30) | data formatting | bytes 8421376 | tf_op jit(solution)/shard_map/while/body/eval_jaxpr/cond/branch_1_fun/reshape | solution.py:11
  346.5 19.5 %conditional.4 = (f32[128,64,16]{0,2,1:T(8,128)S(1)}) conditional(s32[]{:T(128)} %convert_element_type.69, f32[128,64,16]{0,2,1:T(8,128)S(1)} %get-tuple-element.284, (s32[]{:T(128)}, bf16[64,4352]{1,0:T(8,128)(2,1)S(1)}, bf16[32,128,64,16]{1,3,2,0:T(8,128)(2,1)}, s32[]{:T(128)}, f32[128,64,16]{0,2,1:T(8,128)S(1)}) %tuple.50), branch_computations={%region_4.5_spmd, %region_5.6_spmd} | conditional | flops 33685508 | bytes 37176148 | solution.py:102
  349.8 10.9 %reshape.63 = bf16[64,32896]{1,0:T(8,128)(2,1)} reshape(bf16[64,128,257]{2,1,0:T(8,128)(2,1)} %broadcast_in_dim.30) | data formatting | bytes 8421376 | tf_op jit(solution)/shard_map/while/body/eval_jaxpr/cond/branch_1_fun/reshape | solution.py:11
  370.7 19.5 %conditional.4 = (f32[128,64,16]{0,2,1:T(8,128)S(1)}) conditional(s32[]{:T(128)} %convert_element_type.69, f32[128,64,16]{0,2,1:T(8,128)S(1)} %get-tuple-element.284, (s32[]{:T(128)}, bf16[64,4352]{1,0:T(8,128)(2,1)S(1)}, bf16[32,128,64,16]{1,3,2,0:T(8,128)(2,1)}, s32[]{:T(128)}, f32[128,64,16]{0,2,1:T(8,128)S(1)}) %tuple.50), branch_computations={%region_4.5_spmd, %region_5.6_spmd} | conditional | flops 33685508 | bytes 37176148 | solution.py:102
  373.9 10.9 %reshape.63 = bf16[64,32896]{1,0:T(8,128)(2,1)} reshape(bf16[64,128,257]{2,1,0:T(8,128)(2,1)} %broadcast_in_dim.30) | data formatting | bytes 8421376 | tf_op jit(solution)/shard_map/while/body/eval_jaxpr/cond/branch_1_fun/reshape | solution.py:11
  394.8 19.5 %conditional.4 = (f32[128,64,16]{0,2,1:T(8,128)S(1)}) conditional(s32[]{:T(128)} %convert_element_type.69, f32[128,64,16]{0,2,1:T(8,128)S(1)} %get-tuple-element.284, (s32[]{:T(128)}, bf16[64,4352]{1,0:T(8,128)(2,1)S(1)}, bf16[32,128,64,16]{1,3,2,0:T(8,128)(2,1)}, s32[]{:T(128)}, f32[128,64,16]{0,2,1:T(8,128)S(1)}) %tuple.50), branch_computations={%region_4.5_spmd, %region_5.6_spmd} | conditional | flops 33685508 | bytes 37176148 | solution.py:102
  398.0 10.9 %reshape.63 = bf16[64,32896]{1,0:T(8,128)(2,1)} reshape(bf16[64,128,257]{2,1,0:T(8,128)(2,1)} %broadcast_in_dim.30) | data formatting | bytes 8421376 | tf_op jit(solution)/shard_map/while/body/eval_jaxpr/cond/branch_1_fun/reshape | solution.py:11
  418.9 19.5 %conditional.4 = (f32[128,64,16]{0,2,1:T(8,128)S(1)}) conditional(s32[]{:T(128)} %convert_element_type.69, f32[128,64,16]{0,2,1:T(8,128)S(1)} %get-tuple-element.284, (s32[]{:T(128)}, bf16[64,4352]{1,0:T(8,128)(2,1)S(1)}, bf16[32,128,64,16]{1,3,2,0:T(8,128)(2,1)}, s32[]{:T(128)}, f32[128,64,16]{0,2,1:T(8,128)S(1)}) %tuple.50), branch_computations={%region_4.5_spmd, %region_5.6_spmd} | conditional | flops 33685508 | bytes 37176148 | solution.py:102
  443.0 19.5 %conditional.4 = (f32[128,64,16]{0,2,1:T(8,128)S(1)}) conditional(s32[]{:T(128)} %convert_element_type.69, f32[128,64,16]{0,2,1:T(8,128)S(1)} %get-tuple-element.284, (s32[]{:T(128)}, bf16[64,4352]{1,0:T(8,128)(2,1)S(1)}, bf16[32,128,64,16]{1,3,2,0:T(8,128)(2,1)}, s32[]{:T(128)}, f32[128,64,16]{0,2,1:T(8,128)S(1)}) %tuple.50), branch_computations={%region_4.5_spmd, %region_5.6_spmd} | conditional | flops 33685508 | bytes 37176148 | solution.py:102
  467.1 19.5 %conditional.4 = (f32[128,64,16]{0,2,1:T(8,128)S(1)}) conditional(s32[]{:T(128)} %convert_element_type.69, f32[128,64,16]{0,2,1:T(8,128)S(1)} %get-tuple-element.284, (s32[]{:T(128)}, bf16[64,4352]{1,0:T(8,128)(2,1)S(1)}, bf16[32,128,64,16]{1,3,2,0:T(8,128)(2,1)}, s32[]{:T(128)}, f32[128,64,16]{0,2,1:T(8,128)S(1)}) %tuple.50), branch_computations={%region_4.5_spmd, %region_5.6_spmd} | conditional | flops 33685508 | bytes 37176148 | solution.py:102
  491.2 19.5 %conditional.4 = (f32[128,64,16]{0,2,1:T(8,128)S(1)}) conditional(s32[]{:T(128)} %convert_element_type.69, f32[128,64,16]{0,2,1:T(8,128)S(1)} %get-tuple-element.284, (s32[]{:T(128)}, bf16[64,4352]{1,0:T(8,128)(2,1)S(1)}, bf16[32,128,64,16]{1,3,2,0:T(8,128)(2,1)}, s32[]{:T(128)}, f32[128,64,16]{0,2,1:T(8,128)S(1)}) %tuple.50), branch_computations={%region_4.5_spmd, %region_5.6_spmd} | conditional | flops 33685508 | bytes 37176148 | solution.py:102
  515.4 19.5 %conditional.4 = (f32[128,64,16]{0,2,1:T(8,128)S(1)}) conditional(s32[]{:T(128)} %convert_element_type.69, f32[128,64,16]{0,2,1:T(8,128)S(1)} %get-tuple-element.284, (s32[]{:T(128)}, bf16[64,4352]{1,0:T(8,128)(2,1)S(1)}, bf16[32,128,64,16]{1,3,2,0:T(8,128)(2,1)}, s32[]{:T(128)}, f32[128,64,16]{0,2,1:T(8,128)S(1)}) %tuple.50), branch_computations={%region_4.5_spmd, %region_5.6_spmd} | conditional | flops 33685508 | bytes 37176148 | solution.py:102
  518.6 10.9 %reshape.63 = bf16[64,32896]{1,0:T(8,128)(2,1)} reshape(bf16[64,128,257]{2,1,0:T(8,128)(2,1)} %broadcast_in_dim.30) | data formatting | bytes 8421376 | tf_op jit(solution)/shard_map/while/body/eval_jaxpr/cond/branch_1_fun/reshape | solution.py:11
  539.5 19.5 %conditional.4 = (f32[128,64,16]{0,2,1:T(8,128)S(1)}) conditional(s32[]{:T(128)} %convert_element_type.69, f32[128,64,16]{0,2,1:T(8,128)S(1)} %get-tuple-element.284, (s32[]{:T(128)}, bf16[64,4352]{1,0:T(8,128)(2,1)S(1)}, bf16[32,128,64,16]{1,3,2,0:T(8,128)(2,1)}, s32[]{:T(128)}, f32[128,64,16]{0,2,1:T(8,128)S(1)}) %tuple.50), branch_computations={%region_4.5_spmd, %region_5.6_spmd} | conditional | flops 33685508 | bytes 37176148 | solution.py:102
  563.6 19.5 %conditional.4 = (f32[128,64,16]{0,2,1:T(8,128)S(1)}) conditional(s32[]{:T(128)} %convert_element_type.69, f32[128,64,16]{0,2,1:T(8,128)S(1)} %get-tuple-element.284, (s32[]{:T(128)}, bf16[64,4352]{1,0:T(8,128)(2,1)S(1)}, bf16[32,128,64,16]{1,3,2,0:T(8,128)(2,1)}, s32[]{:T(128)}, f32[128,64,16]{0,2,1:T(8,128)S(1)}) %tuple.50), branch_computations={%region_4.5_spmd, %region_5.6_spmd} | conditional | flops 33685508 | bytes 37176148 | solution.py:102
  587.7 19.5 %conditional.4 = (f32[128,64,16]{0,2,1:T(8,128)S(1)}) conditional(s32[]{:T(128)} %convert_element_type.69, f32[128,64,16]{0,2,1:T(8,128)S(1)} %get-tuple-element.284, (s32[]{:T(128)}, bf16[64,4352]{1,0:T(8,128)(2,1)S(1)}, bf16[32,128,64,16]{1,3,2,0:T(8,128)(2,1)}, s32[]{:T(128)}, f32[128,64,16]{0,2,1:T(8,128)S(1)}) %tuple.50), branch_computations={%region_4.5_spmd, %region_5.6_spmd} | conditional | flops 33685508 | bytes 37176148 | solution.py:102
  611.8 19.5 %conditional.4 = (f32[128,64,16]{0,2,1:T(8,128)S(1)}) conditional(s32[]{:T(128)} %convert_element_type.69, f32[128,64,16]{0,2,1:T(8,128)S(1)} %get-tuple-element.284, (s32[]{:T(128)}, bf16[64,4352]{1,0:T(8,128)(2,1)S(1)}, bf16[32,128,64,16]{1,3,2,0:T(8,128)(2,1)}, s32[]{:T(128)}, f32[128,64,16]{0,2,1:T(8,128)S(1)}) %tuple.50), branch_computations={%region_4.5_spmd, %region_5.6_spmd} | conditional | flops 33685508 | bytes 37176148 | solution.py:102
  714.8 214.2 %reduce-scatter.2.cloned.1.call-done = f32[64,128]{1,0:T(8,128)} async-done(((f32[64,4096]{1,0:T(8,128)}), f32[64,128]{1,0:T(8,128)}) %reduce-scatter.2.cloned.1.call-update) | async-done | bytes 32784 | tf_op jit(solution)/shard_map/reduce_scatter | solution.py:114
  (324 shorter events, 390.7 us)
Async XLA Ops:
  7.2 7.0 copy-start
  7.2 14.8 %copy-start.10 = (bf16[128,1024]{1,0:T(8,128)(2,1)S(1)}, bf16[128,1024]{1,0:T(8,128)(2,1)}, u32[]{:S(2)}) copy-start(bf16[128,1024]{1,0:T(8,128)(2,1)} %param.18) | copy-start | bytes 786436
  7.2 28.8 %all-gather.4.cloned.1.call-start = ((), (), s32[]{:S(2)}) async-start(), calls=%async_computation.1 | async-start | bytes 1310720 | tf_op jit(solution)/shard_map/all_gather | solution.py:46
  7.9 92.2 %all-gather.8.cloned.1.call-start = ((), (), s32[]{:S(2)}) async-start(), calls=%async_computation.3 | async-start | bytes 8650752 | tf_op jit(solution)/shard_map/all_gather | solution.py:70
  14.2 11.2 %copy-start.11 = (s32[1024]{0:T(1024)}, s32[1024]{0:T(1024)S(1)}, u32[]{:S(2)}) copy-start(s32[1024]{0:T(1024)S(1)} %get-tuple-element.128) | copy-start | bytes 12292
  14.2 21.9 %copy-start.9 = (bf16[128,1024]{1,0:T(8,128)(2,1)S(1)}, bf16[128,1024]{1,0:T(8,128)(2,1)}, u32[]{:S(2)}) copy-start(bf16[128,1024]{1,0:T(8,128)(2,1)} %param.19) | copy-start | bytes 786436
  22.0 20.7 %copy-start.4 = (bf16[1024,128]{1,0:T(8,128)(2,1)}, bf16[1024,128]{1,0:T(8,128)(2,1)S(1)}, u32[]{:S(2)}) copy-start(bf16[1024,128]{1,0:T(8,128)(2,1)S(1)} %gather_fusion.2) | copy-start | bytes 786436
  25.4 17.3 %copy-start.6 = (bf16[1024,128]{1,0:T(8,128)(2,1)}, bf16[1024,128]{1,0:T(8,128)(2,1)S(1)}, u32[]{:S(2)}) copy-start(bf16[1024,128]{1,0:T(8,128)(2,1)S(1)} %gather_fusion.3) | copy-start | bytes 786436
  26.0 22.3 %copy-start.13 = (pred[1024]{0:T(1024)(128)(4,1)}, pred[1024]{0:T(1024)(128)(4,1)S(1)}, u32[]{:S(2)}) copy-start(pred[1024]{0:T(1024)(128)(4,1)S(1)} %get-tuple-element.197) | copy-start | bytes 3076
  26.9 20.3 %copy-start.16 = (s32[4]{0:T(128)S(1)}, s32[4]{0:T(128)}, u32[]{:S(2)}) copy-start(s32[4]{0:T(128)} %param.24) | copy-start | bytes 52
  26.9 21.3 %copy-start.8 = (bf16[64,4096]{1,0:T(8,128)(2,1)S(1)}, bf16[64,4096]{1,0:T(8,128)(2,1)}, u32[]{:S(2)}) copy-start(bf16[64,4096]{1,0:T(8,128)(2,1)} %param.22) | copy-start | bytes 1572868
  27.0 135.2 %all-gather.6.cloned.1.call-start = ((), (), s32[]{:S(2)}) async-start(), calls=%async_computation.2 | async-start | bytes 8650752 | tf_op jit(solution)/shard_map/all_gather | solution.py:69
  46.1 63.6 %copy-start.2 = (bf16[1024,128]{1,0:T(8,128)(2,1)}, bf16[1024,128]{1,0:T(8,128)(2,1)S(1)}, u32[]{:S(2)}) copy-start(bf16[1024,128]{1,0:T(8,128)(2,1)S(1)} %gather_fusion.1) | copy-start | bytes 786436
  47.0 882.0 %reduce-scatter.2.cloned.1.call-start = ((), (), s32[]{:S(2)}) async-start(), calls=%async_computation.4 | async-start | bytes 1081344 | tf_op jit(solution)/shard_map/reduce_scatter | solution.py:114
  181.7 519.9 %copy-start.12 = (s32[1024]{0:T(1024)S(1)}, s32[1024]{0:T(1024)}, u32[]{:S(2)}) copy-start(s32[1024]{0:T(1024)} %copy-done.11) | copy-start | bytes 12292
  181.7 524.3 %copy-start.3 = (bf16[1024,128]{1,0:T(8,128)(2,1)S(1)}, bf16[1024,128]{1,0:T(8,128)(2,1)}, u32[]{:S(2)}) copy-start(bf16[1024,128]{1,0:T(8,128)(2,1)} %copy-done.2) | copy-start | bytes 786436
  181.7 524.3 %copy-start.5 = (bf16[1024,128]{1,0:T(8,128)(2,1)S(1)}, bf16[1024,128]{1,0:T(8,128)(2,1)}, u32[]{:S(2)}) copy-start(bf16[1024,128]{1,0:T(8,128)(2,1)} %copy-done.4) | copy-start | bytes 786436
  181.7 524.3 %copy-start.7 = (bf16[1024,128]{1,0:T(8,128)(2,1)S(1)}, bf16[1024,128]{1,0:T(8,128)(2,1)}, u32[]{:S(2)}) copy-start(bf16[1024,128]{1,0:T(8,128)(2,1)} %copy-done.6) | copy-start | bytes 786436
  181.8 524.3 %copy-start.14 = (pred[1024]{0:T(1024)(128)(4,1)S(1)}, pred[1024]{0:T(1024)(128)(4,1)}, u32[]{:S(2)}) copy-start(pred[1024]{0:T(1024)(128)(4,1)} %copy-done.13) | copy-start | bytes 3076
  181.8 524.3 %copy-start.15 = (f32[1024]{0:T(1024)S(1)}, f32[1024]{0:T(1024)}, u32[]{:S(2)}) copy-start(f32[1024]{0:T(1024)} %get-tuple-element.196) | copy-start | bytes 12292
  234.4 2.2 slice-start
  288.3 2.2 slice-start
  312.4 2.2 slice-start
  360.7 2.2 slice-start
  384.8 2.2 slice-start
  408.9 2.2 slice-start
  481.2 2.2 slice-start
  505.4 2.2 slice-start
  529.5 2.2 slice-start
  577.7 2.2 slice-start
  601.8 2.2 slice-start
  706.0 223.0 %copy-start.1 = (f32[1024]{0:T(1024)S(1)}, f32[1024]{0:T(1024)}, u32[]{:S(2)}) copy-start(f32[1024]{0:T(1024)} %param.23) | copy-start | bytes 12292
  (5 other events, 10.9 us)
Sparse Core Ops, SparseCore 0:
  9.7 26.2 all-gather.3
  38.8 61.2 all-gather.7
  102.9 59.2 all-gather.5
  701.8 227.2 reduce-scatter.1
where the time goes:
time: 944 us; the launch traced here: 936 us
  local copies, waits for them, and re-layouts  429 us (45%)
  waiting for transfers between devices  318 us (34%)
  loops' own time  108 us (11%)
  matrix products  44.3 us (5%)
  other arithmetic  21.6 us (2%)
  between operations  14.1 us (1%)
    reduce_scatter x1, waiting for transfers between devices, per_device(): lax.psum_scatter(lag_terms, 'ctx', scatter_dimension=1, tiled=True)  214 us
    reshape x16, local copies, waits for them, and re-layouts, skew_rows(): tiled = tiled.reshape(lead + (block_rows * (2 * block_rows + 1),))  174 us
    another operation x1, loops' own time, per_device(): lax.scan(step, carry, (grad_pieces, gate_pieces, jnp.arange(count, dtype=...  106 us
    all_gather x1, waiting for transfers between devices, per_device(): gate_piece = lax.all_gather(gated, 'ctx', axis=0, tiled=True)  51.6 us
    broadcast_in_dim x16, local copies, waits for them, and re-layouts, skew_rows(): jnp.broadcast_to(extended[..., None, :], lead + (block_rows, 2 * block_ro...  51.3 us
    all_gather x1, waiting for transfers between devices, per_device(): grad_piece = lax.all_gather(grad_sorted, 'ctx', axis=0, tiled=True)  42.4 us
    slice x32, local copies, waits for them, and re-layouts, skew_rows(): tiled[..., :2 * block_rows * block_rows]  35 us
    dot_general x16, matrix products, later_work(): jnp.einsum('gst,tgc->sgc', toeplitz, grad_block, preferred_element_type=j...  34.2 us
  transfers between devices with their start and end apart: 4, of which 4 were waited for; matrix products, arithmetic and copies ran while one was open for 7% of the time, Pallas kernels for 0%

commit v1 on v0

v1 whole, which is shorter than its diff:
```python
import jax
import jax.numpy as jnp
from jax import lax
from jax.experimental import pallas as pl
from jax.experimental.pallas import tpu as pltpu
from jax.sharding import PartitionSpec as P

TOK = 128
SPANS = 32
HEADS = 4
CH = 1024
GROUPS = 64
PER = 16
OWN = GROUPS // SPANS
LAGS = 17
KW = LAGS * TOK
HALF = TOK // 2
MESH = pl.DeviceIdType.MESH
F32 = jnp.float32
BF16 = jnp.bfloat16


def dot(a, b, ca, cb):
    return lax.dot_general(a, b, (((ca,), (cb,)), ((), ())), preferred_element_type=F32)


def iota(shape, dim):
    return lax.broadcasted_iota(jnp.int32, shape, dim)


def kernel(
    doc, go, q, k, v, w, filt, grp, skip,
    gq, gk, gf,
    gov, qv, kv, vv, wv, fv, perm, fg, conv, rem, gs, gr, xs, xr, ys, yr, toep, amat, gt, fs, fr,
    loc, ag_send, ag_recv, ex_send, ex_recv,
):
    i = lax.axis_index("ctx")
    h = lax.axis_index("head")
    up = lax.rem(h + 1, HEADS)
    down = lax.rem(h + HEADS - 1, HEADS)
    across = lax.rem(h + 2, HEADS)

    loads = [pltpu.make_async_copy(go, gov.at[0], loc.at[0])]
    loads.append(pltpu.make_async_copy(q, qv, loc.at[1]))
    loads.append(pltpu.make_async_copy(k, kv, loc.at[2]))
    loads.append(pltpu.make_async_copy(v, vv, loc.at[3]))
    loads.append(pltpu.make_async_copy(filt.at[:, pl.ds(0, KW)], fv, loc.at[4]))
    for slot, block in enumerate((h, down, up, across)):
        columns = pl.ds(pl.multiple_of(block * CH, CH), CH)
        loads.append(pltpu.make_async_copy(w.at[:, columns], wv.at[slot], loc.at[5 + slot]))
    for load in loads:
        load.start()

    barrier = pltpu.get_barrier_semaphore()
    pl.semaphore_signal(barrier, inc=1, device_id={"head": up}, device_id_type=MESH)
    pl.semaphore_signal(barrier, inc=1, device_id={"head": down}, device_id_type=MESH)

    def greet(n, carry):
        pl.semaphore_signal(barrier, inc=1, device_id={"ctx": lax.rem(i + n, SPANS)}, device_id_type=MESH)
        return carry

    lax.fori_loop(1, SPANS, greet, 0)
    pl.semaphore_wait(barrier, SPANS + 1)

    low, high = pl.ds(0, HALF), pl.ds(HALF, HALF)

    def over_head(n, src, dst, to):
        return pltpu.make_async_remote_copy(
            src, dst, ag_send.at[n], ag_recv.at[n], device_id={"head": to}, device_id_type=MESH
        )

    gather = [
        over_head(0, go.at[low], gov.at[1, low], up),
        over_head(1, go.at[high], gov.at[2, high], down),
        over_head(2, go.at[high], gov.at[1, high], up),
        over_head(3, go.at[low], gov.at[2, low], down),
        over_head(4, gov.at[1, low], gov.at[3, low], up),
        over_head(5, gov.at[2, high], gov.at[3, high], down),
    ]
    for n in range(4):
        gather[n].start()

    def exchange(n, src, dst, to):
        return pltpu.make_async_remote_copy(
            src, dst, ex_send.at[n], ex_recv.at[n], device_id={"ctx": to}, device_id_type=MESH
        )

    def scatter(n, src, dst):
        def send(step, carry):
            to = lax.rem(i + step, SPANS)
            exchange(n, src.at[to], dst.at[i], to).start()
            return carry

        lax.fori_loop(1, SPANS, send, 0)
        dst[i] = src[i]

    def arrived(n, src, dst):
        exchange(n, src.at[pl.ds(0, SPANS - 1)], dst.at[pl.ds(0, SPANS - 1)], i).wait_recv()

    def sent(n, src, dst):
        exchange(n, src.at[pl.ds(0, SPANS - 1)], dst.at[pl.ds(0, SPANS - 1)], i).wait_send()

    local = grp[...] - h * GROUPS
    before = jnp.where(iota((TOK, TOK), 0) < iota((TOK, TOK), 1), 1.0, 0.0).astype(BF16)
    names = iota((GROUPS, TOK), 0)
    total = jnp.zeros((GROUPS, 1), F32)
    for b in range(CH // TOK):
        row = local[b : b + 1, :]
        hot = jnp.where(names == row, 1.0, 0.0)
        count = jnp.sum(hot * (dot(hot.astype(BF16), before, 1, 0) + total), axis=0, keepdims=True)
        total = total + jnp.sum(hot, axis=1, keepdims=True)
        rank = row * PER + count.astype(jnp.int32)
        for r in range(CH // TOK):
            perm[r * TOK : (r + 1) * TOK, b * TOK : (b + 1) * TOK] = jnp.where(
                iota((TOK, TOK), 0) + r * TOK == rank, 1.0, 0.0
            ).astype(BF16)

    def permuted(rows, out):
        def tile(n, carry):
            part = dot(perm[pl.ds(pl.multiple_of(n * 256, 256), 256), :], rows, 1, 1)
            out[pl.ds(n * 8, 8)] = part.astype(BF16).reshape(8, OWN, PER, TOK)
            return carry

        lax.fori_loop(0, CH // 256, tile, 0)

    loads[1].wait()
    loads[2].wait()
    gated = (qv[...].astype(F32) * kv[...].astype(F32)).astype(BF16)
    permuted(gated, gs)
    scatter(0, gs, gr)

    block = lax.shift_right_logical(iota((SPANS * PER, TOK), 0), 4)
    ends = [doc[0]]
    for n in range(1, 4):
        ends.append(ends[-1] + doc[n])
    end = jnp.where(block < ends[0], ends[0], jnp.where(block < ends[1], ends[1], jnp.where(block < ends[2], ends[2], ends[3])))
    rem[...] = (end - block).astype(F32).astype(BF16).reshape(SPANS, PER, TOK)
    xr[pl.ds(SPANS, LAGS - 1)] = jnp.zeros((LAGS - 1, OWN, PER, TOK), BF16)

    gather[0].wait_recv()
    gather[4].start()
    gather[1].wait_recv()
    gather[5].start()

    def features(slot, first=False):
        def tile(n, carry):
            at = pl.ds(pl.multiple_of(n * 256, 256), 256)
            part = dot(gov[slot], wv[slot, at, :], 1, 1)
            fg[:, at] = part if first else fg[:, at] + part
            return carry

        lax.fori_loop(0, CH // 256, tile, 0)

    loads[0].wait()
    loads[5].wait()
    features(0, True)

    loads[4].wait()
    for u in range(OWN):
        pick = jnp.where(iota((PER, GROUPS), 1) == i * OWN + u, 1.0, 0.0).astype(BF16)
        line = dot(pick, fv[...], 1, 0)
        line = jnp.concatenate([line, jnp.zeros((PER, TOK), F32)], axis=1)
        for c in range(TOK // PER):
            turned = pltpu.roll(line, c * PER, 1, stride=1, stride_axis=0)
            toep[u, c * PER : (c + 1) * PER, :] = turned[:, :KW].astype(BF16)

    gather[2].wait_recv()
    loads[6].wait()
    features(1)
    gather[3].wait_recv()
    loads[7].wait()
    features(2)

    arrived(0, gs, gr)
    flip = jnp.where(iota((TOK, TOK), 0) + iota((TOK, TOK), 1) == TOK - 1, 1.0, 0.0).astype(BF16)
    for u in range(OWN):
        gt[u] = dot(flip, gr[:, u].reshape(SPANS * PER, TOK), 1, 1).astype(BF16)

    gather[4].wait_recv()
    gather[5].wait_recv()
    loads[8].wait()
    features(3)

    loads[3].wait()
    conv[...] = (fg[...] * vv[...].astype(F32)).astype(BF16)
    permuted(conv[...], xs)
    scatter(1, xs, xr)
    arrived(1, xs, xr)

    for u in range(OWN):
        for d in range(LAGS):
            part = jnp.where(rem[...] > d, xr[d : d + SPANS, u], jnp.zeros((), BF16))
            amat[u, :, d * TOK : (d + 1) * TOK] = part.reshape(SPANS * PER, TOK)
        ys[:, u] = dot(amat[u], toep[u], 1, 1).astype(BF16).reshape(SPANS, PER, TOK)
    scatter(2, ys, yr)

    sums = []
    for u in range(OWN):
        acc = jnp.zeros((PER, KW + TOK), F32)
        for c in range(TOK // PER):
            corr = dot(gt[u, c * PER : (c + 1) * PER, :], amat[u], 1, 0)
            corr = jnp.concatenate([corr, jnp.zeros((PER, TOK), F32)], axis=1)
            acc = acc + pltpu.roll(corr, 1 + c * PER, 1, stride=1, stride_axis=0)
        sums.append(jnp.sum(acc, axis=0, keepdims=True)[:, TOK:])
    place = iota((8, TOK), 0) - lax.rem(i, 4) * OWN
    for d in range(LAGS):
        at = slice(d * TOK, (d + 1) * TOK)
        fs[d] = jnp.where(place == 0, sums[0][:, at], jnp.where(place == 1, sums[1][:, at], 0.0))

    def lags_out(step, carry):
        to = lax.rem(i + step, SPANS)

        @pl.when(to < LAGS)
        def _():
            exchange(3, fs.at[to], fr.at[i], to).start()

        return carry

    lax.fori_loop(1, SPANS, lags_out, 0)

    arrived(2, ys, yr)
    for n in range(CH // 256):
        at = slice(n * 256, (n + 1) * 256)
        grad = dot(yr[...].reshape(CH, TOK), perm[:, at], 0, 0)
        grad = grad + skip[:, at] * conv[:, at].astype(F32)
        gq[:, at] = (grad * kv[:, at].astype(F32)).astype(BF16)
        gk[:, at] = (grad * qv[:, at].astype(F32)).astype(BF16)

    @pl.when(i < LAGS)
    def _():
        fr[i] = fs[i]
        arrived(3, fr, fr)
        for n in range(GROUPS // 8):
            gf[n * 8 : (n + 1) * 8, :] = (fr[4 * n] + fr[4 * n + 1]) + (fr[4 * n + 2] + fr[4 * n + 3])
        exchange(3, fs.at[pl.ds(0, LAGS - 1)], fr.at[pl.ds(0, LAGS - 1)], i).wait_send()

    @pl.when(i >= LAGS)
    def _():
        gf[...] = jnp.zeros((GROUPS, TOK), F32)
        exchange(3, fs, fr.at[pl.ds(0, LAGS)], i).wait_send()

    for copy in gather:
        copy.wait_send()
    sent(0, gs, gr)
    sent(1, xs, xr)
    sent(2, ys, yr)


def per_device(
    query_proj, key_proj, value_proj, grad_out, out_proj, filters, skip_gain, doc_lengths, group_of
):
    hbm = pl.BlockSpec(memory_space=pl.ANY)
    vmem = pl.BlockSpec(memory_space=pltpu.VMEM)
    smem = pl.BlockSpec(memory_space=pltpu.SMEM)
    dma = pltpu.SemaphoreType.DMA
    blocks = (SPANS, OWN, PER, TOK)
    return pl.pallas_call(
        kernel,
        out_shape=(
            jax.ShapeDtypeStruct((TOK, CH), BF16),
            jax.ShapeDtypeStruct((TOK, CH), BF16),
            jax.ShapeDtypeStruct((GROUPS, TOK), F32),
        ),
        in_specs=[smem, hbm, hbm, hbm, hbm, hbm, hbm, vmem, vmem],
        out_specs=(vmem, vmem, vmem),
        scratch_shapes=[
            pltpu.VMEM((HEADS, TOK, CH), BF16),
            pltpu.VMEM((TOK, CH), BF16),
            pltpu.VMEM((TOK, CH), BF16),
            pltpu.VMEM((TOK, CH), BF16),
            pltpu.VMEM((HEADS, CH, CH), BF16),
            pltpu.VMEM((GROUPS, KW), BF16),
            pltpu.VMEM((CH, CH), BF16),
            pltpu.VMEM((TOK, CH), F32),
            pltpu.VMEM((TOK, CH), BF16),
            pltpu.VMEM((SPANS, PER, TOK), BF16),
            pltpu.VMEM(blocks, BF16),
            pltpu.VMEM(blocks, BF16),
            pltpu.VMEM(blocks, BF16),
            pltpu.VMEM((SPANS + LAGS - 1, OWN, PER, TOK), BF16),
            pltpu.VMEM(blocks, BF16),
            pltpu.VMEM(blocks, BF16),
            pltpu.VMEM((OWN, TOK, KW), BF16),
            pltpu.VMEM((OWN, SPANS * PER, KW), BF16),
            pltpu.VMEM((OWN, TOK, SPANS * PER), BF16),
            pltpu.VMEM((LAGS, 8, TOK), F32),
            pltpu.VMEM((SPANS, 8, TOK), F32),
            dma((9,)),
            dma((6,)),
            dma((6,)),
            dma((4,)),
            dma((4,)),
        ],
        compiler_params=pltpu.CompilerParams(
            collective_id=0, has_side_effects=True, vmem_limit_bytes=48 << 20
        ),
    )(
        doc_lengths, grad_out, query_proj, key_proj, value_proj, out_proj, filters,
        group_of.reshape(CH // TOK, TOK), skip_gain.reshape(1, CH),
    )


def solution(mesh):
    in_specs = (
        P("ctx", "head"),
        P("ctx", "head"),
        P("ctx", "head"),
        P("ctx", "head"),
        P("head", None),
        P("head", None),
        P("head"),
        P(),
        P("head"),
    )
    out_specs = (P("ctx", "head"), P("ctx", "head"), P("head", "ctx"))
    return jax.shard_map(
        per_device, mesh=mesh, in_specs=in_specs, out_specs=out_specs, check_vma=False
    )
```

time: 944 us -> 51.9 us (0.05)
  local copies, waits for them, and re-layouts: 429 us -> 8.88 us
  waiting for transfers between devices: 318 us -> 0 us
  loops' own time: 108 us -> 0 us
  matrix products: 44.3 us -> 0 us
  Pallas kernels: 0 us -> 42 us
  other arithmetic: 21.6 us -> 0 us
  between operations: 14.1 us -> 0.66 us
    reduce_scatter x1 -> x0, waiting for transfers between devices: 214 us -> none  [per_device(): lax.psum_scatter(lag_terms, 'ctx', scatter_dimension=1, tiled=True)]
    reshape x18 -> x0, local copies, waits for them, and re-layouts: 202 us -> none  [the longest x16 174 us: skew_rows(): tiled = tiled.reshape(lead + (block_rows * (2 * block_rows + 1),))]
    another operation x65 -> x0, loops' own time: 108 us -> none  [the longest x1 106 us: per_device(): lax.scan(step, carry, (grad_pieces, gate_pieces, jnp.arange(count, dtype=...]
    all_gather x3 -> x0, waiting for transfers between devices: 103 us -> none  [the longest x1 51.6 us: per_device(): gate_piece = lax.all_gather(gated, 'ctx', axis=0, tiled=True)]
    broadcast_in_dim x19 -> x0, local copies, waits for them, and re-layouts: 51.4 us -> none  [the longest x16 51.3 us: skew_rows(): jnp.broadcast_to(extended[..., None, :], lead + (block_rows, 2 * block_ro...]
    dot_general x19 -> x0, matrix products: 44.3 us -> none  [the longest x16 34.2 us: later_work(): jnp.einsum('gst,tgc->sgc', toeplitz, grad_block, preferred_element_type=j...]
    pallas_call x0 -> x1, Pallas kernels: none -> 42 us  [per_device(): pl.pallas_call(kernel, out_shape=(jax.ShapeDtypeStruct((TOK, CH), BF16),...]
    dynamic_slice x81 -> x0, local copies, waits for them, and re-layouts: 40.4 us -> none  [the longest x32 20.8 us: step(): same = span_doc[jnp.clip(offset, 0, spans - 1)] == own_doc]
  transfers between devices with their start and end apart: 4 -> 0, of which waited for: 4 -> 0; matrix products, arithmetic and copies ran while one was open for 7% -> 0% of each run, Pallas kernels for 0% -> 0%
where the time goes in v1:
time: 51.9 us; the launch traced here: 51.5 us
  Pallas kernels  42 us (81%)
  local copies, waits for them, and re-layouts  8.88 us (17%)
  between operations  0.66 us (1%)
    pallas_call x1, Pallas kernels, per_device(): pl.pallas_call(kernel, out_shape=(jax.ShapeDtypeStruct((TOK, CH), BF16),...  42 us
    unnamed x19, local copies, waits for them, and re-layouts  8.88 us

profile of v1, /device:TPU:1, one launch (start us, length us, event | category | flops | bytes accessed | tf_op | source)
XLA Modules:
  0.0 51.5 jit_solution(3120146622101873441)
XLA Ops:
  0.6 0.0 copy-start
  0.6 1.0 %copy-done = bf16[64,4096]{1,0:T(8,128)(2,1)S(1)} copy-done((bf16[64,4096]{1,0:T(8,128)(2,1)S(1)}, bf16[64,4096]{1,0:T(8,128)(2,1)}, u32[]{:S(2)}) %copy-start) | copy-done | bytes 524312
  1.7 0.0 copy-start.1
  1.7 0.9 %copy-done.1 = bf16[128,1024]{1,0:T(8,128)(2,1)S(1)} copy-done((bf16[128,1024]{1,0:T(8,128)(2,1)S(1)}, bf16[128,1024]{1,0:T(8,128)(2,1)}, u32[]{:S(2)}) %copy-start.1) | copy-done | bytes 262168
  2.6 0.0 copy-start.2
  2.6 0.9 %copy-done.2 = bf16[128,1024]{1,0:T(8,128)(2,1)S(1)} copy-done((bf16[128,1024]{1,0:T(8,128)(2,1)S(1)}, bf16[128,1024]{1,0:T(8,128)(2,1)}, u32[]{:S(2)}) %copy-start.2) | copy-done | bytes 262168
  3.6 0.0 copy-start.3
  3.6 0.9 %copy-done.3 = bf16[128,1024]{1,0:T(8,128)(2,1)S(1)} copy-done((bf16[128,1024]{1,0:T(8,128)(2,1)S(1)}, bf16[128,1024]{1,0:T(8,128)(2,1)}, u32[]{:S(2)}) %copy-start.3) | copy-done | bytes 262168
  4.5 0.0 copy-start.4
  4.5 0.9 %copy-done.4 = bf16[128,1024]{1,0:T(8,128)(2,1)S(1)} copy-done((bf16[128,1024]{1,0:T(8,128)(2,1)S(1)}, bf16[128,1024]{1,0:T(8,128)(2,1)}, u32[]{:S(2)}) %copy-start.4) | copy-done | bytes 262168
  5.5 0.0 copy-start.5
  5.5 0.7 %copy-done.5 = s32[1024]{0:T(1024)S(1)} copy-done((s32[1024]{0:T(1024)S(1)}, s32[1024]{0:T(1024)}, u32[]{:S(2)}) %copy-start.5) | copy-done | bytes 4120
  6.2 0.0 copy-start.6
  6.2 0.7 %copy-done.6 = f32[1024]{0:T(1024)S(1)} copy-done((f32[1024]{0:T(1024)S(1)}, f32[1024]{0:T(1024)}, u32[]{:S(2)}) %copy-start.6) | copy-done | bytes 4120
  6.9 0.0 copy-start.7
  6.9 0.7 %copy-done.7 = s32[4]{0:T(128)S(1)} copy-done((s32[4]{0:T(128)S(1)}, s32[4]{0:T(128)}, u32[]{:S(2)}) %copy-start.7) | copy-done | bytes 40
  7.5 42.0 %shard_map.112 = (bf16[128,1024]{1,0:T(8,128)(2,1)S(1)}, bf16[128,1024]{1,0:T(8,128)(2,1)S(1)}, f32[64,128]{1,0:T(8,128)S(1)}) custom-call(s32[4]{0:T(128)S(1)} %copy-done.7, bf16[128,1024]{1,0:T(8,128)(2,1)S(1)} %copy-done.1, bf16[128,1024]{1,0:T(8,128)(2,1)S(1)} %copy-done.2, bf16[128,1024]{1,0:T(8,128)(2,1)S(1)} %copy-done.3, ...), custom_call_target="tpu_custom_call" | custom-call | tf_op jit(solution)/shard_map/pallas_call | solution.py:257
  49.5 0.7 %copy.15 = bf16[128,1024]{1,0:T(8,128)(2,1)} copy(bf16[128,1024]{1,0:T(8,128)(2,1)S(1)} %get-tuple-element.6) | data formatting | bytes 524288
  50.2 0.7 %copy.16 = bf16[128,1024]{1,0:T(8,128)(2,1)} copy(bf16[128,1024]{1,0:T(8,128)(2,1)S(1)} %get-tuple-element.7) | data formatting | bytes 524288
  50.9 0.6 %copy.17 = f32[64,128]{1,0:T(8,128)} copy(f32[64,128]{1,0:T(8,128)S(1)} %get-tuple-element.8) | data formatting | bytes 65536
Async XLA Ops:
  0.6 1.0 %copy-start = (bf16[64,4096]{1,0:T(8,128)(2,1)S(1)}, bf16[64,4096]{1,0:T(8,128)(2,1)}, u32[]{:S(2)}) copy-start(bf16[64,4096]{1,0:T(8,128)(2,1)} %filt.1) | copy-start | bytes 1572868
  1.7 0.9 %copy-start.1 = (bf16[128,1024]{1,0:T(8,128)(2,1)S(1)}, bf16[128,1024]{1,0:T(8,128)(2,1)}, u32[]{:S(2)}) copy-start(bf16[128,1024]{1,0:T(8,128)(2,1)} %go.1) | copy-start | bytes 786436
  2.6 0.9 %copy-start.2 = (bf16[128,1024]{1,0:T(8,128)(2,1)S(1)}, bf16[128,1024]{1,0:T(8,128)(2,1)}, u32[]{:S(2)}) copy-start(bf16[128,1024]{1,0:T(8,128)(2,1)} %q.1) | copy-start | bytes 786436
  3.6 0.9 %copy-start.3 = (bf16[128,1024]{1,0:T(8,128)(2,1)S(1)}, bf16[128,1024]{1,0:T(8,128)(2,1)}, u32[]{:S(2)}) copy-start(bf16[128,1024]{1,0:T(8,128)(2,1)} %k.1) | copy-start | bytes 786436
  4.5 0.9 %copy-start.4 = (bf16[128,1024]{1,0:T(8,128)(2,1)S(1)}, bf16[128,1024]{1,0:T(8,128)(2,1)}, u32[]{:S(2)}) copy-start(bf16[128,1024]{1,0:T(8,128)(2,1)} %v.1) | copy-start | bytes 786436
  5.5 0.7 %copy-start.5 = (s32[1024]{0:T(1024)S(1)}, s32[1024]{0:T(1024)}, u32[]{:S(2)}) copy-start(s32[1024]{0:T(1024)} %param.17) | copy-start | bytes 12292
  6.2 0.7 %copy-start.6 = (f32[1024]{0:T(1024)S(1)}, f32[1024]{0:T(1024)}, u32[]{:S(2)}) copy-start(f32[1024]{0:T(1024)} %param.15) | copy-start | bytes 12292
  6.9 0.7 %copy-start.7 = (s32[4]{0:T(128)S(1)}, s32[4]{0:T(128)}, u32[]{:S(2)}) copy-start(s32[4]{0:T(128)} %doc.1) | copy-start | bytes 52

commit v2 on v1

v2 whole, which is shorter than its diff:
```python
import jax
import jax.numpy as jnp
from jax import lax
from jax.experimental import pallas as pl
from jax.experimental.pallas import tpu as pltpu
from jax.sharding import PartitionSpec as P

TOK = 128
SPANS = 32
HEADS = 4
CH = 1024
GROUPS = 64
PER = 16
OWN = GROUPS // SPANS
LAGS = 17
KW = LAGS * TOK
HALF = SPANS // 2
PIECE = CH // 4
ROWS = SPANS * PER
MESH = pl.DeviceIdType.MESH
F32 = jnp.float32
BF16 = jnp.bfloat16


def dot(a, b, ca, cb):
    return lax.dot_general(a, b, (((ca,), (cb,)), ((), ())), preferred_element_type=F32)


def iota(shape, dim):
    return lax.broadcasted_iota(jnp.int32, shape, dim)


def kernel(
    doc_in, go, q, k, v, w, filt, grp_in, skip_in,
    yr, perm, conv, qv, kv, skip, fr,
    own, gov, vv, wv, fv, grp, doc, fg, rem, gs, gr, xs, xr, ys, toep, amat, gt, corr, fs,
    loc, ag_send, ag_recv, ex_send, ex_recv,
):
    i = lax.axis_index("ctx")
    h = lax.axis_index("head")
    up = lax.rem(h + 1, HEADS)
    down = lax.rem(h + HEADS - 1, HEADS)
    across = lax.rem(h + 2, HEADS)
    x, z, core = i // 8, lax.rem(i // 2, 4), lax.rem(i, 2)

    barrier = pltpu.get_barrier_semaphore()
    pl.semaphore_signal(barrier, inc=1, device_id={"head": up}, device_id_type=MESH)
    pl.semaphore_signal(barrier, inc=1, device_id={"head": down}, device_id_type=MESH)

    def greet(n, carry):
        pl.semaphore_signal(barrier, inc=1, device_id={"ctx": lax.rem(i + n, SPANS)}, device_id_type=MESH)
        return carry

    lax.fori_loop(1, SPANS, greet, 0)

    pairs = [(grp_in, grp), (go, own), (q, qv), (k, kv), (doc_in, doc), (filt.at[:, pl.ds(0, KW)], fv), (v, vv), (skip_in, skip)]
    for slot, block in enumerate((h, down, up, across)):
        pairs.append((w.at[:, pl.ds(pl.multiple_of(block * CH, CH), CH)], wv.at[slot]))
    loads = [pltpu.make_async_copy(src, dst, loc.at[n]) for n, (src, dst) in enumerate(pairs)]
    for load in loads:
        load.start()
    l_grp, l_own, l_q, l_k, l_doc, l_filt, l_v, l_skip = loads[:8]
    l_w = loads[8:]
    pl.semaphore_wait(barrier, SPANS + 1)

    def over_head(n, src, dst, to, first, count):
        at = pl.ds(first * PIECE, count * PIECE)
        return pltpu.make_async_remote_copy(
            src.at[:, at], dst.at[:, at], ag_send.at[n], ag_recv.at[n], device_id={"head": to}, device_id_type=MESH
        )

    to_up = [over_head(0, go, gov.at[0], up, 0, 1), over_head(1, go, gov.at[0], up, 1, 1), over_head(2, go, gov.at[0], up, 2, 2)]
    to_down = [over_head(3, go, gov.at[1], down, 2, 1), over_head(4, go, gov.at[1], down, 3, 1), over_head(5, go, gov.at[1], down, 0, 2)]
    on_up = [over_head(6 + n, gov.at[0], gov.at[2], up, n, 1) for n in range(2)]
    on_down = [over_head(8 + n, gov.at[1], gov.at[2], down, 2 + n, 1) for n in range(2)]
    for n in range(2):
        to_up[n].start()
        to_down[n].start()

    flips = {0: x, 1: x + 1 - 2 * lax.rem(x, 2), 2: lax.rem(x + 2, 4), 3: 3 - x}
    turns = {0: z, 1: z + 1 - 2 * lax.rem(z, 2), 2: lax.rem(z + 2, 4), 3: 3 - z}
    hops = {0: 0, 1: 1, 2: 2, 3: 1}
    sides = []
    for side in ((2, 3), (1, 0)):
        steps = [(a, b, c) for a in side for b in range(4) for c in range(2) if a or b or c]
        steps.sort(key=lambda e: -hops[e[0]] - hops[e[1]])
        sides.append([flips[a] * 8 + turns[b] * 2 + (core if c == 0 else 1 - core) for a, b, c in steps])
    halves = (1 - x // 2, x // 2)

    def exchange(n, src, dst, to):
        return pltpu.make_async_remote_copy(
            src, dst, ex_send.at[n], ex_recv.at[n], device_id={"ctx": to}, device_id_type=MESH
        )

    def everything(n, src, dst):
        return exchange(n, src.at[pl.ds(0, SPANS - 1)], dst.at[pl.ds(0, SPANS - 1)], i)

    l_grp.wait()
    local = grp[...] - h * GROUPS
    before = jnp.where(iota((TOK, TOK), 0) < iota((TOK, TOK), 1), 1.0, 0.0).astype(BF16)
    names = iota((GROUPS, TOK), 0)
    total = jnp.zeros((GROUPS, 1), F32)
    for b in range(CH // TOK):
        row = local[b : b + 1, :]
        hot = jnp.where(names == row, 1.0, 0.0)
        count = jnp.sum(hot * (dot(hot.astype(BF16), before, 1, 0) + total), axis=0, keepdims=True)
        total = total + jnp.sum(hot, axis=1, keepdims=True)
        rank = (row & (OWN - 1)) * ROWS + lax.shift_right_logical(row, 1) * PER + count.astype(jnp.int32)
        for r in range(CH // TOK):
            perm[r * TOK : (r + 1) * TOK, b * TOK : (b + 1) * TOK] = jnp.where(
                iota((TOK, TOK), 0) + r * TOK == rank, 1.0, 0.0
            ).astype(BF16)

    l_q.wait()
    l_k.wait()
    gated = (qv[...].astype(F32) * kv[...].astype(F32)).astype(BF16)
    for u in range(OWN):
        gs[u] = dot(perm[u * ROWS : (u + 1) * ROWS, :], gated, 1, 1).astype(BF16).reshape(SPANS, PER, TOK)
    for side in sides:
        for to in side:
            exchange(0, gs.at[:, to], gr.at[:, i], to).start()
    gr[:, i] = gs[:, i]

    to_up[2].start()
    to_down[2].start()

    def features(block, slot, first=False):
        def tile(n, carry):
            at = pl.ds(pl.multiple_of(n * 256, 256), 256)
            part = dot(block[...], wv[slot, at, :], 1, 1)
            fg[:, at] = part if first else fg[:, at] + part
            return carry

        lax.fori_loop(0, CH // 256, tile, 0)

    l_own.wait()
    l_w[0].wait()
    features(own, 0, True)

    for n in range(2):
        to_up[n].wait_recv()
        on_up[n].start()
        to_down[n].wait_recv()
        on_down[n].start()

    l_doc.wait()
    block = lax.shift_right_logical(iota((ROWS, TOK), 0), 4)
    ends = [doc[0]]
    for n in range(1, 4):
        ends.append(ends[-1] + doc[n])
    end = jnp.where(block < ends[0], ends[0], jnp.where(block < ends[1], ends[1], jnp.where(block < ends[2], ends[2], ends[3])))
    rem[...] = (end - block).astype(F32).astype(BF16).reshape(SPANS, PER, TOK)
    xr[:, SPANS:] = jnp.zeros((OWN, LAGS - 1, PER, TOK), BF16)
    corr[:, KW:] = jnp.zeros((TOK, TOK), F32)

    l_filt.wait()
    for u in range(OWN):
        pick = jnp.where(iota((PER, GROUPS), 1) == i * OWN + u, 1.0, 0.0).astype(BF16)
        line = dot(pick, fv[...], 1, 0)
        line = jnp.concatenate([line, jnp.zeros((PER, TOK), F32)], axis=1)
        for c in range(TOK // PER):
            turned = pltpu.roll(line, c * PER, 1, stride=1, stride_axis=0)
            toep[u, c * PER : (c + 1) * PER, :] = turned[:, :KW].astype(BF16)

    to_up[2].wait_recv()
    l_w[1].wait()
    features(gov.at[0], 1)
    to_down[2].wait_recv()
    l_w[2].wait()
    features(gov.at[1], 2)

    exchange(0, gs.at[:, pl.ds(0, SPANS - 1)], gr.at[:, pl.ds(0, SPANS - 1)], i).wait_recv()
    flip = jnp.where(iota((TOK, TOK), 0) + iota((TOK, TOK), 1) == TOK - 1, 1.0, 0.0).astype(BF16)
    for u in range(OWN):
        gt[u] = dot(flip, gr[u].reshape(ROWS, TOK), 1, 1).astype(BF16)

    l_w[3].wait()
    l_v.wait()
    far = gov.at[2]
    for n in range(2):
        on_up[n].wait_recv()
        on_down[n].wait_recv()
        one, two = pl.ds(n * PIECE, PIECE), pl.ds((2 + n) * PIECE, PIECE)

        def tile(m, carry):
            at = pl.ds(pl.multiple_of(m * 256, 256), 256)
            part = dot(far[:, one], wv[3, at, one], 1, 1) + dot(far[:, two], wv[3, at, two], 1, 1)
            if n == 0:
                fg[:, at] = fg[:, at] + part
            else:
                conv[:, at] = ((fg[:, at] + part) * vv[:, at].astype(F32)).astype(BF16)
            return carry

        lax.fori_loop(0, CH // 256, tile, 0)

    for u in range(OWN):
        for side, half in zip(sides, halves):
            at = pl.ds(pl.multiple_of(u * ROWS + half * (ROWS // 2), ROWS // 2), ROWS // 2)
            part = dot(perm[at, :], conv[...], 1, 1)
            xs[u, pl.ds(half * HALF, HALF)] = part.astype(BF16).reshape(HALF, PER, TOK)
            for to in side:
                exchange(1 + u, xs.at[u, to], xr.at[u, i], to).start()
        xr[u, i] = xs[u, i]

    for u in range(OWN):
        everything(1 + u, xs.at[u], xr.at[u]).wait_recv()
        for side, half in zip(sides, halves):
            rows = pl.ds(pl.multiple_of(half * (ROWS // 2), ROWS // 2), ROWS // 2)
            for d in range(LAGS):
                near = rem[pl.ds(half * HALF, HALF)] > d
                part = jnp.where(near, xr[u, pl.ds(half * HALF + d, HALF)], jnp.zeros((), BF16))
                amat[u, rows, d * TOK : (d + 1) * TOK] = part.reshape(ROWS // 2, TOK)
            part = dot(amat[u, rows, :], toep[u], 1, 1)
            ys[u, pl.ds(half * HALF, HALF)] = part.astype(BF16).reshape(HALF, PER, TOK)
            for to in side:
                exchange(3 + u, ys.at[u, to], yr.at[u, i], to).start()
        yr[u, i] = ys[u, i]

    for u in range(OWN):
        corr[:, :KW] = dot(gt[u], amat[u], 1, 0)
        acc = jnp.zeros((PER, KW + TOK), F32)
        for c in range(TOK // PER):
            acc = acc + pltpu.roll(corr[c * PER : (c + 1) * PER, :], 1 + c * PER, 1, stride=1, stride_axis=0)
        line = jnp.sum(acc, axis=0, keepdims=True)
        for d in range(LAGS):
            fs[d, u : u + 1, :] = line[:, (d + 1) * TOK : (d + 2) * TOK]

    def lags_out(step, carry):
        to = lax.rem(i + step, SPANS)

        @pl.when(to < LAGS)
        def _():
            exchange(5, fs.at[to], fr.at[i], to).start()

        return carry

    lax.fori_loop(1, SPANS, lags_out, 0)

    @pl.when(i < LAGS)
    def _():
        fr[i] = fs[i]
        everything(5, fr, fr).wait_recv()
        exchange(5, fs.at[pl.ds(0, LAGS - 1)], fr.at[pl.ds(0, LAGS - 1)], i).wait_send()

    @pl.when(i >= LAGS)
    def _():
        fr[...] = jnp.zeros(fr.shape, F32)
        exchange(5, fs, fr.at[pl.ds(0, LAGS)], i).wait_send()

    for copy in (*to_up, *to_down, *on_up, *on_down):
        copy.wait_send()
    exchange(0, gs.at[:, pl.ds(0, SPANS - 1)], gr.at[:, pl.ds(0, SPANS - 1)], i).wait_send()
    l_skip.wait()
    for u in range(OWN):
        everything(1 + u, xs.at[u], xr.at[u]).wait_send()
        everything(3 + u, ys.at[u], yr.at[u]).wait_send()
        everything(3 + u, ys.at[u], yr.at[u]).wait_recv()


def finish(yr, perm, conv, qv, kv, skip, fr, gq, gk, gf, out_q, out_k, out_f, sem):
    for t in range(SPANS):
        out_f[t * OWN : (t + 1) * OWN, :] = fr[t]
    copies = [pltpu.make_async_copy(out_f, gf, sem.at[0])]
    copies[0].start()
    for n in range(CH // 256):
        at = slice(n * 256, (n + 1) * 256)
        grad = dot(yr[...].reshape(CH, TOK), perm[:, at], 0, 0)
        grad = grad + skip[:, at] * conv[:, at].astype(F32)
        out_q[:, at] = (grad * kv[:, at].astype(F32)).astype(BF16)
        out_k[:, at] = (grad * qv[:, at].astype(F32)).astype(BF16)
        for m, (src, dst) in enumerate(((out_q, gq), (out_k, gk))):
            copies.append(pltpu.make_async_copy(src.at[:, at], dst.at[:, at], sem.at[1 + 2 * n + m]))
            copies[-1].start()
    for copy in copies:
        copy.wait()


def per_device(
    query_proj, key_proj, value_proj, grad_out, out_proj, filters, skip_gain, doc_lengths, group_of
):
    hbm = pl.BlockSpec(memory_space=pltpu.HBM)
    vmem = pl.BlockSpec(memory_space=pltpu.VMEM)
    dma = pltpu.SemaphoreType.DMA
    blocks = (OWN, SPANS, PER, TOK)
    rows = (TOK, CH)
    args = (
        doc_lengths, grad_out, query_proj, key_proj, value_proj, out_proj, filters,
        group_of.reshape(CH // TOK, TOK), skip_gain.reshape(1, CH),
    )
    held = pl.pallas_call(
        kernel,
        out_shape=(
            jax.ShapeDtypeStruct(blocks, BF16),
            jax.ShapeDtypeStruct((CH, CH), BF16),
            jax.ShapeDtypeStruct(rows, BF16),
            jax.ShapeDtypeStruct(rows, BF16),
            jax.ShapeDtypeStruct(rows, BF16),
            jax.ShapeDtypeStruct((1, CH), F32),
            jax.ShapeDtypeStruct((SPANS, OWN, TOK), F32),
        ),
        in_specs=[hbm] * 9,
        out_specs=(vmem,) * 7,
        scratch_shapes=[
            pltpu.VMEM(rows, BF16),
            pltpu.VMEM((HEADS - 1, *rows), BF16),
            pltpu.VMEM(rows, BF16),
            pltpu.VMEM((HEADS, CH, CH), BF16),
            pltpu.VMEM((GROUPS, KW), BF16),
            pltpu.VMEM((CH // TOK, TOK), jnp.int32),
            pltpu.SMEM((4,), jnp.int32),
            pltpu.VMEM(rows, F32),
            pltpu.VMEM((SPANS, PER, TOK), BF16),
            pltpu.VMEM(blocks, BF16),
            pltpu.VMEM(blocks, BF16),
            pltpu.VMEM(blocks, BF16),
            pltpu.VMEM((OWN, SPANS + LAGS - 1, PER, TOK), BF16),
            pltpu.VMEM(blocks, BF16),
            pltpu.VMEM((OWN, TOK, KW), BF16),
            pltpu.VMEM((OWN, ROWS, KW), BF16),
            pltpu.VMEM((OWN, TOK, ROWS), BF16),
            pltpu.VMEM((TOK, KW + TOK), F32),
            pltpu.VMEM((LAGS, OWN, TOK), F32),
            dma((12,)),
            dma((10,)),
            dma((10,)),
            dma((6,)),
            dma((6,)),
        ],
        compiler_params=pltpu.CompilerParams(
            collective_id=0, has_side_effects=True, vmem_limit_bytes=40 << 20
        ),
    )(*(pltpu.with_memory_space_constraint(arg, pltpu.HBM) for arg in args))
    return pl.pallas_call(
        finish,
        out_shape=(
            jax.ShapeDtypeStruct(rows, BF16),
            jax.ShapeDtypeStruct(rows, BF16),
            jax.ShapeDtypeStruct((GROUPS, TOK), F32),
        ),
        in_specs=[vmem] * 7,
        out_specs=(hbm,) * 3,
        scratch_shapes=[pltpu.VMEM(rows, BF16), pltpu.VMEM(rows, BF16), pltpu.VMEM((GROUPS, TOK), F32), dma((9,))],
        compiler_params=pltpu.CompilerParams(vmem_limit_bytes=16 << 20),
    )(*held)


def solution(mesh):
    in_specs = (
        P("ctx", "head"),
        P("ctx", "head"),
        P("ctx", "head"),
        P("ctx", "head"),
        P("head", None),
        P("head", None),
        P("head"),
        P(),
        P("head"),
    )
    out_specs = (P("ctx", "head"), P("ctx", "head"), P("head", "ctx"))
    return jax.shard_map(
        per_device, mesh=mesh, in_specs=in_specs, out_specs=out_specs, check_vma=False
    )
```

time: 51.9 us -> 39.1 us (0.75)
  local copies, waits for them, and re-layouts: 8.88 us -> 0 us
  Pallas kernels: 42 us -> 38.4 us
    unnamed x19 -> x0, local copies, waits for them, and re-layouts: 8.88 us -> none
    pallas_call x1 -> x2, Pallas kernels: 42 us -> 38.4 us  [the longest x1 37.1 us: per_device(): pl.pallas_call(kernel, out_shape=(jax.ShapeDtypeStruct(blocks, BF16), jax...]
where the time goes in v2:
time: 39.1 us; the launch traced here: 39 us
  Pallas kernels  38.4 us (98%)
  between operations  0.64 us (2%)
    pallas_call x1, Pallas kernels, per_device(): pl.pallas_call(kernel, out_shape=(jax.ShapeDtypeStruct(blocks, BF16), jax...  37.1 us
    pallas_call x1, Pallas kernels, per_device(): pl.pallas_call(finish, out_shape=(jax.ShapeDtypeStruct(rows, BF16), jax.S...  1.28 us

profile of v2, /device:TPU:1, one launch (start us, length us, event | category | flops | bytes accessed | tf_op | source)
XLA Modules:
  0.0 39.0 jit_solution(15048644753139340137)
XLA Ops:
  0.6 37.1 %shard_map.112 = (bf16[2,32,16,128]{3,2,1,0:T(8,128)(2,1)S(1)}, bf16[1024,1024]{1,0:T(8,128)(2,1)S(1)}, bf16[128,1024]{1,0:T(8,128)(2,1)S(1)}, bf16[128,1024]{1,...) custom-call(s32[4]{0:T(128)} %doc_in.1, ...), custom_call_target="tpu_custom_call" | custom-call | tf_op jit(solution)/shard_map/pallas_call | solution.py:290
  37.7 1.3 %shard_map.113 = (bf16[128,1024]{1,0:T(8,128)(2,1)}, bf16[128,1024]{1,0:T(8,128)(2,1)}, f32[64,128]{1,0:T(8,128)}) custom-call(bf16[2,32,16,128]{3,2,1,0:T(8,128)(2,1)S(1)} %get-tuple-element.10.yr, bf16[1024,1024]{1,0:T(8,128)(2,1)S(1)} %get-tuple-element.11.perm, bf16[128,1024]{1,0:T(8,128)(2,1)S(1)} %get-tuple-element.12.conv, ...), custom_call_target="tpu_custom_call" | custom-call | tf_op jit(solution)/shard_map/pallas_call | solution.py:333

commit v3 on v2

--- a/solution.py
+++ b/solution.py
@@ -15,7 +15,7 @@
 LAGS = 17
 KW = LAGS * TOK
 HALF = SPANS // 2
-PIECE = CH // 4
+PIECE = CH // 8
 ROWS = SPANS * PER
 MESH = pl.DeviceIdType.MESH
 F32 = jnp.float32
@@ -32,8 +32,8 @@
 
 def kernel(
     doc_in, go, q, k, v, w, filt, grp_in, skip_in,
-    yr, perm, conv, qv, kv, skip, fr,
-    own, gov, vv, wv, fv, grp, doc, fg, rem, gs, gr, xs, xr, ys, toep, amat, gt, corr, fs,
+    out_q, out_k, fr,
+    yr, perm, conv, qv, kv, skip, own, gov, vv, wv, fv, grp, doc, fg, rem, gs, gr, xs, xr, ys, toep, amat, gt, corr, fs,
     loc, ag_send, ag_recv, ex_send, ex_recv,
 ):
     i = lax.axis_index("ctx")
@@ -69,11 +69,14 @@
             src.at[:, at], dst.at[:, at], ag_send.at[n], ag_recv.at[n], device_id={"head": to}, device_id_type=MESH
         )
 
-    to_up = [over_head(0, go, gov.at[0], up, 0, 1), over_head(1, go, gov.at[0], up, 1, 1), over_head(2, go, gov.at[0], up, 2, 2)]
-    to_down = [over_head(3, go, gov.at[1], down, 2, 1), over_head(4, go, gov.at[1], down, 3, 1), over_head(5, go, gov.at[1], down, 0, 2)]
-    on_up = [over_head(6 + n, gov.at[0], gov.at[2], up, n, 1) for n in range(2)]
-    on_down = [over_head(8 + n, gov.at[1], gov.at[2], down, 2 + n, 1) for n in range(2)]
-    for n in range(2):
+    first, second = range(4), range(4, 8)
+    to_up = [over_head(n, go, gov.at[0], up, n, 1) for n in first]
+    to_down = [over_head(n, go, gov.at[1], down, n, 1) for n in second]
+    rest_up = over_head(8, go, gov.at[0], up, 4, 4)
+    rest_down = over_head(9, go, gov.at[1], down, 0, 4)
+    on_up = [over_head(10 + n, gov.at[0], gov.at[2], up, n, 1) for n in first]
+    on_down = [over_head(10 + n, gov.at[1], gov.at[2], down, n, 1) for n in second]
+    for n in first:
         to_up[n].start()
         to_down[n].start()
 
@@ -121,8 +124,8 @@
             exchange(0, gs.at[:, to], gr.at[:, i], to).start()
     gr[:, i] = gs[:, i]
 
-    to_up[2].start()
-    to_down[2].start()
+    rest_up.start()
+    rest_down.start()
 
     def features(block, slot, first=False):
         def tile(n, carry):
@@ -137,7 +140,7 @@
     l_w[0].wait()
     features(own, 0, True)
 
-    for n in range(2):
+    for n in first:
         to_up[n].wait_recv()
         on_up[n].start()
         to_down[n].wait_recv()
@@ -162,36 +165,35 @@
             turned = pltpu.roll(line, c * PER, 1, stride=1, stride_axis=0)
             toep[u, c * PER : (c + 1) * PER, :] = turned[:, :KW].astype(BF16)
 
-    to_up[2].wait_recv()
+    rest_up.wait_recv()
     l_w[1].wait()
     features(gov.at[0], 1)
-    to_down[2].wait_recv()
+    rest_down.wait_recv()
     l_w[2].wait()
     features(gov.at[1], 2)
 
     exchange(0, gs.at[:, pl.ds(0, SPANS - 1)], gr.at[:, pl.ds(0, SPANS - 1)], i).wait_recv()
     flip = jnp.where(iota((TOK, TOK), 0) + iota((TOK, TOK), 1) == TOK - 1, 1.0, 0.0).astype(BF16)
     for u in range(OWN):
-        gt[u] = dot(flip, gr[u].reshape(ROWS, TOK), 1, 1).astype(BF16)
+        for p, half in enumerate(halves):
+            rows = gr[u, pl.ds(half * HALF, HALF)].reshape(ROWS // 2, TOK)
+            gt[u, p] = dot(flip, rows, 1, 1).astype(BF16)
 
     l_w[3].wait()
     l_v.wait()
     far = gov.at[2]
-    for n in range(2):
+    for n in first:
         on_up[n].wait_recv()
         on_down[n].wait_recv()
-        one, two = pl.ds(n * PIECE, PIECE), pl.ds((2 + n) * PIECE, PIECE)
-
-        def tile(m, carry):
-            at = pl.ds(pl.multiple_of(m * 256, 256), 256)
-            part = dot(far[:, one], wv[3, at, one], 1, 1) + dot(far[:, two], wv[3, at, two], 1, 1)
-            if n == 0:
-                fg[:, at] = fg[:, at] + part
+        one, two = pl.ds(n * PIECE, PIECE), pl.ds((4 + n) * PIECE, PIECE)
+        rows = jnp.concatenate([far[:, one], far[:, two]], axis=1)
+        for m in range(CH // 256):
+            at = slice(m * 256, (m + 1) * 256)
+            part = fg[:, at] + dot(rows, jnp.concatenate([wv[3, at, one], wv[3, at, two]], axis=1), 1, 1)
+            if n < 3:
+                fg[:, at] = part
             else:
-                conv[:, at] = ((fg[:, at] + part) * vv[:, at].astype(F32)).astype(BF16)
-            return carry
-
-        lax.fori_loop(0, CH // 256, tile, 0)
+                conv[:, at] = (part * vv[:, at].astype(F32)).astype(BF16)
 
     for u in range(OWN):
         for side, half in zip(sides, halves):
@@ -204,37 +206,50 @@
 
     for u in range(OWN):
         everything(1 + u, xs.at[u], xr.at[u]).wait_recv()
-        for side, half in zip(sides, halves):
-            rows = pl.ds(pl.multiple_of(half * (ROWS // 2), ROWS // 2), ROWS // 2)
-            for d in range(LAGS):
-                near = rem[pl.ds(half * HALF, HALF)] > d
-                part = jnp.where(near, xr[u, pl.ds(half * HALF + d, HALF)], jnp.zeros((), BF16))
-                amat[u, rows, d * TOK : (d + 1) * TOK] = part.reshape(ROWS // 2, TOK)
-            part = dot(amat[u, rows, :], toep[u], 1, 1)
-            ys[u, pl.ds(half * HALF, HALF)] = part.astype(BF16).reshape(HALF, PER, TOK)
+        for p, (side, half) in enumerate(zip(sides, halves)):
+            left = rem[pl.ds(half * HALF, HALF)]
+            acc = jnp.zeros((ROWS // 2, TOK), F32)
+            for d in range(0, LAGS, 2):
+                parts = [
+                    jnp.where(left > e, xr[u, pl.ds(half * HALF + e, HALF)], jnp.zeros((), BF16)).reshape(ROWS // 2, TOK)
+                    for e in range(d, min(d + 2, LAGS))
+                ]
+                at = slice(d * TOK, (d + len(parts)) * TOK)
+                part = jnp.concatenate(parts, axis=1)
+                amat[u, p, :, at] = part
+                acc = acc + dot(part, toep[u, :, at], 1, 1)
+            ys[u, pl.ds(half * HALF, HALF)] = acc.astype(BF16).reshape(HALF, PER, TOK)
             for to in side:
                 exchange(3 + u, ys.at[u, to], yr.at[u, i], to).start()
         yr[u, i] = ys[u, i]
 
     for u in range(OWN):
-        corr[:, :KW] = dot(gt[u], amat[u], 1, 0)
+        corr[:, :KW] = dot(gt[u, 0], amat[u, 0], 1, 0) + dot(gt[u, 1], amat[u, 1], 1, 0)
         acc = jnp.zeros((PER, KW + TOK), F32)
         for c in range(TOK // PER):
             acc = acc + pltpu.roll(corr[c * PER : (c + 1) * PER, :], 1 + c * PER, 1, stride=1, stride_axis=0)
         line = jnp.sum(acc, axis=0, keepdims=True)
         for d in range(LAGS):
             fs[d, u : u + 1, :] = line[:, (d + 1) * TOK : (d + 2) * TOK]
-
-    def lags_out(step, carry):
-        to = lax.rem(i + step, SPANS)
-
-        @pl.when(to < LAGS)
-        def _():
-            exchange(5, fs.at[to], fr.at[i], to).start()
-
-        return carry
-
-    lax.fori_loop(1, SPANS, lags_out, 0)
+    for side in sides:
+        for to in side:
+
+            @pl.when(to < LAGS)
+            def _(to=to):
+                exchange(5, fs.at[to], fr.at[i], to).start()
+
+    l_skip.wait()
+    for u in range(OWN):
+        everything(3 + u, ys.at[u], yr.at[u]).wait_recv()
+        for n in range(CH // 256):
+            at = slice(n * 256, (n + 1) * 256)
+            part = dot(yr[u].reshape(ROWS, TOK), perm[u * ROWS : (u + 1) * ROWS, at], 0, 0)
+            if u == 0:
+                fg[:, at] = part + skip[:, at] * conv[:, at].astype(F32)
+            else:
+                grad = fg[:, at] + part
+                out_q[:, at] = (grad * kv[:, at].astype(F32)).astype(BF16)
+                out_k[:, at] = (grad * qv[:, at].astype(F32)).astype(BF16)
 
     @pl.when(i < LAGS)
     def _():
@@ -247,30 +262,21 @@
         fr[...] = jnp.zeros(fr.shape, F32)
         exchange(5, fs, fr.at[pl.ds(0, LAGS)], i).wait_send()
 
-    for copy in (*to_up, *to_down, *on_up, *on_down):
+    for copy in (*to_up, *to_down, rest_up, rest_down, *on_up, *on_down):
         copy.wait_send()
     exchange(0, gs.at[:, pl.ds(0, SPANS - 1)], gr.at[:, pl.ds(0, SPANS - 1)], i).wait_send()
-    l_skip.wait()
     for u in range(OWN):
         everything(1 + u, xs.at[u], xr.at[u]).wait_send()
         everything(3 + u, ys.at[u], yr.at[u]).wait_send()
-        everything(3 + u, ys.at[u], yr.at[u]).wait_recv()
-
-
-def finish(yr, perm, conv, qv, kv, skip, fr, gq, gk, gf, out_q, out_k, out_f, sem):
+
+
+def finish(out_q, out_k, fr, gq, gk, gf, out_f, sem):
+    copies = [pltpu.make_async_copy(src, dst, sem.at[n]) for n, (src, dst) in enumerate(((out_q, gq), (out_k, gk), (out_f, gf)))]
+    copies[0].start()
+    copies[1].start()
     for t in range(SPANS):
         out_f[t * OWN : (t + 1) * OWN, :] = fr[t]
-    copies = [pltpu.make_async_copy(out_f, gf, sem.at[0])]
-    copies[0].start()
-    for n in range(CH // 256):
-        at = slice(n * 256, (n + 1) * 256)
-        grad = dot(yr[...].reshape(CH, TOK), perm[:, at], 0, 0)
-        grad = grad + skip[:, at] * conv[:, at].astype(F32)
-        out_q[:, at] = (grad * kv[:, at].astype(F32)).astype(BF16)
-        out_k[:, at] = (grad * qv[:, at].astype(F32)).astype(BF16)
-        for m, (src, dst) in enumerate(((out_q, gq), (out_k, gk))):
-            copies.append(pltpu.make_async_copy(src.at[:, at], dst.at[:, at], sem.at[1 + 2 * n + m]))
-            copies[-1].start()
+    copies[2].start()
     for copy in copies:
         copy.wait()
 
@@ -290,17 +296,19 @@
     held = pl.pallas_call(
         kernel,
         out_shape=(
-            jax.ShapeDtypeStruct(blocks, BF16),
-            jax.ShapeDtypeStruct((CH, CH), BF16),
             jax.ShapeDtypeStruct(rows, BF16),
             jax.ShapeDtypeStruct(rows, BF16),
-            jax.ShapeDtypeStruct(rows, BF16),
-            jax.ShapeDtypeStruct((1, CH), F32),
             jax.ShapeDtypeStruct((SPANS, OWN, TOK), F32),
         ),
         in_specs=[hbm] * 9,
-        out_specs=(vmem,) * 7,
+        out_specs=(vmem,) * 3,
         scratch_shapes=[
+            pltpu.VMEM(blocks, BF16),
+            pltpu.VMEM((CH, CH), BF16),
+            pltpu.VMEM(rows, BF16),
+            pltpu.VMEM(rows, BF16),
+            pltpu.VMEM(rows, BF16),
+            pltpu.VMEM((1, CH), F32),
             pltpu.VMEM(rows, BF16),
             pltpu.VMEM((HEADS - 1, *rows), BF16),
             pltpu.VMEM(rows, BF16),
@@ -316,13 +324,13 @@
             pltpu.VMEM((OWN, SPANS + LAGS - 1, PER, TOK), BF16),
             pltpu.VMEM(blocks, BF16),
             pltpu.VMEM((OWN, TOK, KW), BF16),
-            pltpu.VMEM((OWN, ROWS, KW), BF16),
-            pltpu.VMEM((OWN, TOK, ROWS), BF16),
+            pltpu.VMEM((OWN, 2, ROWS // 2, KW), BF16),
+            pltpu.VMEM((OWN, 2, TOK, ROWS // 2), BF16),
             pltpu.VMEM((TOK, KW + TOK), F32),
             pltpu.VMEM((LAGS, OWN, TOK), F32),
             dma((12,)),
-            dma((10,)),
-            dma((10,)),
+            dma((18,)),
+            dma((18,)),
             dma((6,)),
             dma((6,)),
         ],
@@ -337,9 +345,9 @@
             jax.ShapeDtypeStruct(rows, BF16),
             jax.ShapeDtypeStruct((GROUPS, TOK), F32),
         ),
-        in_specs=[vmem] * 7,
+        in_specs=[vmem] * 3,
         out_specs=(hbm,) * 3,
-        scratch_shapes=[pltpu.VMEM(rows, BF16), pltpu.VMEM(rows, BF16), pltpu.VMEM((GROUPS, TOK), F32), dma((9,))],
+        scratch_shapes=[pltpu.VMEM((GROUPS, TOK), F32), dma((3,))],
         compiler_params=pltpu.CompilerParams(vmem_limit_bytes=16 << 20),
     )(*held)
 

time: 39.1 us -> 37.8 us (0.967)
  Pallas kernels: 38.4 us -> 37.1 us
    pallas_call x1, Pallas kernels: 37.1 us -> 36.3 us  [per_device(): pl.pallas_call(kernel, out_shape=(jax.ShapeDtypeStruct(rows, BF16), jax.S...]
    pallas_call x1, Pallas kernels: 1.28 us -> 0.82 us  [per_device(): pl.pallas_call(finish, out_shape=(jax.ShapeDtypeStruct(rows, BF16), jax.S...]
where the time goes in v3:
time: 37.8 us; the launch traced here: 37.7 us
  Pallas kernels  37.1 us (98%)
  between operations  0.64 us (2%)
    pallas_call x1, Pallas kernels, per_device(): pl.pallas_call(kernel, out_shape=(jax.ShapeDtypeStruct(rows, BF16), jax.S...  36.3 us
    pallas_call x1, Pallas kernels, per_device(): pl.pallas_call(finish, out_shape=(jax.ShapeDtypeStruct(rows, BF16), jax.S...  0.82 us

profile of v3, /device:TPU:1, one launch (start us, length us, event | category | flops | bytes accessed | tf_op | source)
XLA Modules:
  0.0 37.7 jit_solution(13855568814111173383)
XLA Ops:
  0.6 36.3 %shard_map.112 = (bf16[128,1024]{1,0:T(8,128)(2,1)S(1)}, bf16[128,1024]{1,0:T(8,128)(2,1)S(1)}, f32[32,2,128]{2,1,0:T(2,128)S(1)}) custom-call(s32[4]{0:T(128)} %doc_in.1, bf16[128,1024]{1,0:T(8,128)(2,1)} %go.1, bf16[128,1024]{1,0:T(8,128)(2,1)} %q.1, bf16[128,1024]{1,0:T(8,128)(2,1)} %k.1, bf16[128,1024]{1,0:T(8,128)(2,1)} %v.1, bf16[1024,4096]{1,0:T(8,128)(2,1)} %w.1, ...), custom_call_target="tpu_custom_call" | custom-call | tf_op jit(solution)/shard_map/pallas_call | solution.py:296
  36.9 0.8 %shard_map.113 = (bf16[128,1024]{1,0:T(8,128)(2,1)}, bf16[128,1024]{1,0:T(8,128)(2,1)}, f32[64,128]{1,0:T(8,128)}) custom-call(bf16[128,1024]{1,0:T(8,128)(2,1)S(1)} %get-tuple-element.6.out_q, bf16[128,1024]{1,0:T(8,128)(2,1)S(1)} %get-tuple-element.7.out_k, f32[32,2,128]{2,1,0:T(2,128)S(1)} %get-tuple-element.8.fr), custom_call_target="tpu_custom_call" | custom-call | tf_op jit(solution)/shard_map/pallas_call | solution.py:341

commit v4 on v3

--- a/solution.py
+++ b/solution.py
@@ -70,12 +70,13 @@
         )
 
     first, second = range(4), range(4, 8)
-    to_up = [over_head(n, go, gov.at[0], up, n, 1) for n in first]
-    to_down = [over_head(n, go, gov.at[1], down, n, 1) for n in second]
-    rest_up = over_head(8, go, gov.at[0], up, 4, 4)
-    rest_down = over_head(9, go, gov.at[1], down, 0, 4)
+    to_up = [over_head(n, own, gov.at[0], up, n, 1) for n in first]
+    to_down = [over_head(n, own, gov.at[1], down, n, 1) for n in second]
+    rest_up = over_head(8, own, gov.at[0], up, 4, 4)
+    rest_down = over_head(9, own, gov.at[1], down, 0, 4)
     on_up = [over_head(10 + n, gov.at[0], gov.at[2], up, n, 1) for n in first]
     on_down = [over_head(10 + n, gov.at[1], gov.at[2], down, n, 1) for n in second]
+    l_own.wait()
     for n in first:
         to_up[n].start()
         to_down[n].start()
@@ -83,20 +84,23 @@
     flips = {0: x, 1: x + 1 - 2 * lax.rem(x, 2), 2: lax.rem(x + 2, 4), 3: 3 - x}
     turns = {0: z, 1: z + 1 - 2 * lax.rem(z, 2), 2: lax.rem(z + 2, 4), 3: 3 - z}
     hops = {0: 0, 1: 1, 2: 2, 3: 1}
-    sides = []
-    for side in ((2, 3), (1, 0)):
-        steps = [(a, b, c) for a in side for b in range(4) for c in range(2) if a or b or c]
-        steps.sort(key=lambda e: -hops[e[0]] - hops[e[1]])
-        sides.append([flips[a] * 8 + turns[b] * 2 + (core if c == 0 else 1 - core) for a, b, c in steps])
+
+    def by_distance(steps):
+        steps = sorted(steps, key=lambda e: -hops[e[0]] - hops[e[1]])
+        return [flips[a] * 8 + turns[b] * 2 + (core if c == 0 else 1 - core) for a, b, c in steps]
+
     halves = (1 - x // 2, x // 2)
+    steps = [(a, b, c) for a in range(4) for b in range(4) for c in range(2) if a or b or c]
+    partners = by_distance(steps)
+    sides = [by_distance([e for e in steps if (e[0] > 1) == far]) for far in (True, False)]
 
     def exchange(n, src, dst, to):
         return pltpu.make_async_remote_copy(
             src, dst, ex_send.at[n], ex_recv.at[n], device_id={"ctx": to}, device_id_type=MESH
         )
 
-    def everything(n, src, dst):
-        return exchange(n, src.at[pl.ds(0, SPANS - 1)], dst.at[pl.ds(0, SPANS - 1)], i)
+    def both(n, src, dst):
+        return exchange(n, src.at[:, pl.ds(0, SPANS - 1)], dst.at[:, pl.ds(0, SPANS - 1)], i)
 
     l_grp.wait()
     local = grp[...] - h * GROUPS
@@ -119,9 +123,8 @@
     gated = (qv[...].astype(F32) * kv[...].astype(F32)).astype(BF16)
     for u in range(OWN):
         gs[u] = dot(perm[u * ROWS : (u + 1) * ROWS, :], gated, 1, 1).astype(BF16).reshape(SPANS, PER, TOK)
-    for side in sides:
-        for to in side:
-            exchange(0, gs.at[:, to], gr.at[:, i], to).start()
+    for to in partners:
+        exchange(0, gs.at[:, to], gr.at[:, i], to).start()
     gr[:, i] = gs[:, i]
 
     rest_up.start()
@@ -136,7 +139,6 @@
 
         lax.fori_loop(0, CH // 256, tile, 0)
 
-    l_own.wait()
     l_w[0].wait()
     features(own, 0, True)
 
@@ -172,7 +174,7 @@
     l_w[2].wait()
     features(gov.at[1], 2)
 
-    exchange(0, gs.at[:, pl.ds(0, SPANS - 1)], gr.at[:, pl.ds(0, SPANS - 1)], i).wait_recv()
+    both(0, gs, gr).wait_recv()
     flip = jnp.where(iota((TOK, TOK), 0) + iota((TOK, TOK), 1) == TOK - 1, 1.0, 0.0).astype(BF16)
     for u in range(OWN):
         for p, half in enumerate(halves):
@@ -196,18 +198,16 @@
                 conv[:, at] = (part * vv[:, at].astype(F32)).astype(BF16)
 
     for u in range(OWN):
-        for side, half in zip(sides, halves):
-            at = pl.ds(pl.multiple_of(u * ROWS + half * (ROWS // 2), ROWS // 2), ROWS // 2)
-            part = dot(perm[at, :], conv[...], 1, 1)
-            xs[u, pl.ds(half * HALF, HALF)] = part.astype(BF16).reshape(HALF, PER, TOK)
-            for to in side:
-                exchange(1 + u, xs.at[u, to], xr.at[u, i], to).start()
-        xr[u, i] = xs[u, i]
-
-    for u in range(OWN):
-        everything(1 + u, xs.at[u], xr.at[u]).wait_recv()
-        for p, (side, half) in enumerate(zip(sides, halves)):
-            left = rem[pl.ds(half * HALF, HALF)]
+        part = dot(perm[u * ROWS : (u + 1) * ROWS, :], conv[...], 1, 1)
+        xs[u] = part.astype(BF16).reshape(SPANS, PER, TOK)
+    for to in partners:
+        exchange(1, xs.at[:, to], xr.at[:, i], to).start()
+    xr[:, i] = xs[:, i]
+
+    both(1, xs, xr).wait_recv()
+    for p, (side, half) in enumerate(zip(sides, halves)):
+        left = rem[pl.ds(half * HALF, HALF)]
+        for u in range(OWN):
             acc = jnp.zeros((ROWS // 2, TOK), F32)
             for d in range(0, LAGS, 2):
                 parts = [
@@ -219,9 +219,9 @@
                 amat[u, p, :, at] = part
                 acc = acc + dot(part, toep[u, :, at], 1, 1)
             ys[u, pl.ds(half * HALF, HALF)] = acc.astype(BF16).reshape(HALF, PER, TOK)
-            for to in side:
-                exchange(3 + u, ys.at[u, to], yr.at[u, i], to).start()
-        yr[u, i] = ys[u, i]
+        for to in side:
+            exchange(2, ys.at[:, to], yr.at[:, i], to).start()
+    yr[:, i] = ys[:, i]
 
     for u in range(OWN):
         corr[:, :KW] = dot(gt[u, 0], amat[u, 0], 1, 0) + dot(gt[u, 1], amat[u, 1], 1, 0)
@@ -236,11 +236,11 @@
 
             @pl.when(to < LAGS)
             def _(to=to):
-                exchange(5, fs.at[to], fr.at[i], to).start()
+                exchange(3, fs.at[to], fr.at[i], to).start()
 
     l_skip.wait()
-    for u in range(OWN):
-        everything(3 + u, ys.at[u], yr.at[u]).wait_recv()
+    both(2, ys, yr).wait_recv()
+    for u in range(OWN):
         for n in range(CH // 256):
             at = slice(n * 256, (n + 1) * 256)
             part = dot(yr[u].reshape(ROWS, TOK), perm[u * ROWS : (u + 1) * ROWS, at], 0, 0)
@@ -254,20 +254,19 @@
     @pl.when(i < LAGS)
     def _():
         fr[i] = fs[i]
-        everything(5, fr, fr).wait_recv()
-        exchange(5, fs.at[pl.ds(0, LAGS - 1)], fr.at[pl.ds(0, LAGS - 1)], i).wait_send()
+        exchange(3, fr.at[pl.ds(0, SPANS - 1)], fr.at[pl.ds(0, SPANS - 1)], i).wait_recv()
+        exchange(3, fs.at[pl.ds(0, LAGS - 1)], fr.at[pl.ds(0, LAGS - 1)], i).wait_send()
 
     @pl.when(i >= LAGS)
     def _():
         fr[...] = jnp.zeros(fr.shape, F32)
-        exchange(5, fs, fr.at[pl.ds(0, LAGS)], i).wait_send()
+        exchange(3, fs, fr.at[pl.ds(0, LAGS)], i).wait_send()
 
     for copy in (*to_up, *to_down, rest_up, rest_down, *on_up, *on_down):
         copy.wait_send()
-    exchange(0, gs.at[:, pl.ds(0, SPANS - 1)], gr.at[:, pl.ds(0, SPANS - 1)], i).wait_send()
-    for u in range(OWN):
-        everything(1 + u, xs.at[u], xr.at[u]).wait_send()
-        everything(3 + u, ys.at[u], yr.at[u]).wait_send()
+    both(0, gs, gr).wait_send()
+    both(1, xs, xr).wait_send()
+    both(2, ys, yr).wait_send()
 
 
 def finish(out_q, out_k, fr, gq, gk, gf, out_f, sem):
@@ -331,8 +330,8 @@
             dma((12,)),
             dma((18,)),
             dma((18,)),
-            dma((6,)),
-            dma((6,)),
+            dma((4,)),
+            dma((4,)),
         ],
         compiler_params=pltpu.CompilerParams(
             collective_id=0, has_side_effects=True, vmem_limit_bytes=40 << 20

time: 37.8 us -> 37.2 us (0.984)
  Pallas kernels: 37.1 us -> 36.5 us
    pallas_call x1, Pallas kernels: 36.3 us -> 35.6 us  [per_device(): pl.pallas_call(kernel, out_shape=(jax.ShapeDtypeStruct(rows, BF16), jax.S...]
where the time goes in v4:
time: 37.2 us; the launch traced here: 37.1 us
  Pallas kernels  36.5 us (98%)
  between operations  0.64 us (2%)
    pallas_call x1, Pallas kernels, per_device(): pl.pallas_call(kernel, out_shape=(jax.ShapeDtypeStruct(rows, BF16), jax.S...  35.6 us
    pallas_call x1, Pallas kernels, per_device(): pl.pallas_call(finish, out_shape=(jax.ShapeDtypeStruct(rows, BF16), jax.S...  0.82 us

profile of v4, /device:TPU:1, one launch (start us, length us, event | category | flops | bytes accessed | tf_op | source)
XLA Modules:
  0.0 37.1 jit_solution(10837739107665567471)
XLA Ops:
  0.6 35.6 %shard_map.112 = (bf16[128,1024]{1,0:T(8,128)(2,1)S(1)}, bf16[128,1024]{1,0:T(8,128)(2,1)S(1)}, f32[32,2,128]{2,1,0:T(2,128)S(1)}) custom-call(s32[4]{0:T(128)} %doc_in.1, bf16[128,1024]{1,0:T(8,128)(2,1)} %go.1, bf16[128,1024]{1,0:T(8,128)(2,1)} %q.1, bf16[128,1024]{1,0:T(8,128)(2,1)} %k.1, bf16[128,1024]{1,0:T(8,128)(2,1)} %v.1, bf16[1024,4096]{1,0:T(8,128)(2,1)} %w.1, ...), custom_call_target="tpu_custom_call" | custom-call | tf_op jit(solution)/shard_map/pallas_call | solution.py:295
  36.3 0.8 %shard_map.113 = (bf16[128,1024]{1,0:T(8,128)(2,1)}, bf16[128,1024]{1,0:T(8,128)(2,1)}, f32[64,128]{1,0:T(8,128)}) custom-call(bf16[128,1024]{1,0:T(8,128)(2,1)S(1)} %get-tuple-element.6.out_q, bf16[128,1024]{1,0:T(8,128)(2,1)S(1)} %get-tuple-element.7.out_k, f32[32,2,128]{2,1,0:T(2,128)S(1)} %get-tuple-element.8.fr), custom_call_target="tpu_custom_call" | custom-call | tf_op jit(solution)/shard_map/pallas_call | solution.py:340

commit v5 on v4

--- a/solution.py
+++ b/solution.py
@@ -33,7 +33,7 @@
 def kernel(
     doc_in, go, q, k, v, w, filt, grp_in, skip_in,
     out_q, out_k, fr,
-    yr, perm, conv, qv, kv, skip, own, gov, vv, wv, fv, grp, doc, fg, rem, gs, gr, xs, xr, ys, toep, amat, gt, corr, fs,
+    yr, perm, conv, qv, kv, skip, own, gov, vv, wv, fv, grp, doc, fg, rem, gs, gr, xs, xr, ys, toep, amat, gt, corr, fs, gain,
     loc, ag_send, ag_recv, ex_send, ex_recv,
 ):
     i = lax.axis_index("ctx")
@@ -158,6 +158,11 @@
     xr[:, SPANS:] = jnp.zeros((OWN, LAGS - 1, PER, TOK), BF16)
     corr[:, KW:] = jnp.zeros((TOK, TOK), F32)
 
+    l_skip.wait()
+    for u in range(OWN):
+        hot = perm[pl.ds(pl.multiple_of(u * ROWS + i * PER, PER), PER), :].astype(F32)
+        gain[u] = jnp.broadcast_to(jnp.sum(hot * skip[...], axis=1, keepdims=True), (PER, TOK))
+
     l_filt.wait()
     for u in range(OWN):
         pick = jnp.where(iota((PER, GROUPS), 1) == i * OWN + u, 1.0, 0.0).astype(BF16)
@@ -208,7 +213,7 @@
     for p, (side, half) in enumerate(zip(sides, halves)):
         left = rem[pl.ds(half * HALF, HALF)]
         for u in range(OWN):
-            acc = jnp.zeros((ROWS // 2, TOK), F32)
+            acc = (xr[u, pl.ds(half * HALF, HALF)].astype(F32) * gain[u][None]).reshape(ROWS // 2, TOK)
             for d in range(0, LAGS, 2):
                 parts = [
                     jnp.where(left > e, xr[u, pl.ds(half * HALF + e, HALF)], jnp.zeros((), BF16)).reshape(ROWS // 2, TOK)
@@ -238,14 +243,13 @@
             def _(to=to):
                 exchange(3, fs.at[to], fr.at[i], to).start()
 
-    l_skip.wait()
     both(2, ys, yr).wait_recv()
     for u in range(OWN):
         for n in range(CH // 256):
             at = slice(n * 256, (n + 1) * 256)
             part = dot(yr[u].reshape(ROWS, TOK), perm[u * ROWS : (u + 1) * ROWS, at], 0, 0)
             if u == 0:
-                fg[:, at] = part + skip[:, at] * conv[:, at].astype(F32)
+                fg[:, at] = part
             else:
                 grad = fg[:, at] + part
                 out_q[:, at] = (grad * kv[:, at].astype(F32)).astype(BF16)
@@ -327,6 +331,7 @@
             pltpu.VMEM((OWN, 2, TOK, ROWS // 2), BF16),
             pltpu.VMEM((TOK, KW + TOK), F32),
             pltpu.VMEM((LAGS, OWN, TOK), F32),
+            pltpu.VMEM((OWN, PER, TOK), F32),
             dma((12,)),
             dma((18,)),
             dma((18,)),

time: 37.2 us -> 37.2 us (level)
  no operation moved by 1% of the time
where the time goes in v5:
time: 37.2 us; the launch traced here: 37.1 us
  Pallas kernels  36.5 us (98%)
  between operations  0.64 us (2%)
    pallas_call x1, Pallas kernels, per_device(): pl.pallas_call(kernel, out_shape=(jax.ShapeDtypeStruct(rows, BF16), jax.S...  35.6 us
    pallas_call x1, Pallas kernels, per_device(): pl.pallas_call(finish, out_shape=(jax.ShapeDtypeStruct(rows, BF16), jax.S...  0.82 us

profile of v5, /device:TPU:1, one launch (start us, length us, event | category | flops | bytes accessed | tf_op | source)
XLA Modules:
  0.0 37.1 jit_solution(10376281343054662826)
XLA Ops:
  0.6 35.6 %shard_map.112 = (bf16[128,1024]{1,0:T(8,128)(2,1)S(1)}, bf16[128,1024]{1,0:T(8,128)(2,1)S(1)}, f32[32,2,128]{2,1,0:T(2,128)S(1)}) custom-call(s32[4]{0:T(128)} %doc_in.1, bf16[128,1024]{1,0:T(8,128)(2,1)} %go.1, bf16[128,1024]{1,0:T(8,128)(2,1)} %q.1, bf16[128,1024]{1,0:T(8,128)(2,1)} %k.1, bf16[128,1024]{1,0:T(8,128)(2,1)} %v.1, bf16[1024,4096]{1,0:T(8,128)(2,1)} %w.1, ...), custom_call_target="tpu_custom_call" | custom-call | tf_op jit(solution)/shard_map/pallas_call | solution.py:299
  36.3 0.8 %shard_map.113 = (bf16[128,1024]{1,0:T(8,128)(2,1)}, bf16[128,1024]{1,0:T(8,128)(2,1)}, f32[64,128]{1,0:T(8,128)}) custom-call(bf16[128,1024]{1,0:T(8,128)(2,1)S(1)} %get-tuple-element.6.out_q, bf16[128,1024]{1,0:T(8,128)(2,1)S(1)} %get-tuple-element.7.out_k, f32[32,2,128]{2,1,0:T(2,128)S(1)} %get-tuple-element.8.fr), custom_call_target="tpu_custom_call" | custom-call | tf_op jit(solution)/shard_map/pallas_call | solution.py:345

commit v6 on v5

--- a/solution.py
+++ b/solution.py
@@ -80,6 +80,8 @@
     for n in first:
         to_up[n].start()
         to_down[n].start()
+    rest_up.start()
+    rest_down.start()
 
     flips = {0: x, 1: x + 1 - 2 * lax.rem(x, 2), 2: lax.rem(x + 2, 4), 3: 3 - x}
     turns = {0: z, 1: z + 1 - 2 * lax.rem(z, 2), 2: lax.rem(z + 2, 4), 3: 3 - z}
@@ -127,8 +129,6 @@
         exchange(0, gs.at[:, to], gr.at[:, i], to).start()
     gr[:, i] = gs[:, i]
 
-    rest_up.start()
-    rest_down.start()
 
     def features(block, slot, first=False):
         def tile(n, carry):
@@ -211,12 +211,16 @@
 
     both(1, xs, xr).wait_recv()
     for p, (side, half) in enumerate(zip(sides, halves)):
-        left = rem[pl.ds(half * HALF, HALF)]
+        left = []
+        for m in range(HALF):
+            j = half * HALF + m
+            e0 = jnp.where(j < ends[0], ends[0], jnp.where(j < ends[1], ends[1], jnp.where(j < ends[2], ends[2], ends[3])))
+            left.append(e0 - j)
         for u in range(OWN):
             acc = (xr[u, pl.ds(half * HALF, HALF)].astype(F32) * gain[u][None]).reshape(ROWS // 2, TOK)
             for d in range(0, LAGS, 2):
                 parts = [
-                    jnp.where(left > e, xr[u, pl.ds(half * HALF + e, HALF)], jnp.zeros((), BF16)).reshape(ROWS // 2, TOK)
+                    jnp.concatenate([jnp.where(left[m] > e, xr[u, half * HALF + (e + m)], jnp.zeros((PER, TOK), BF16)) for m in range(HALF)], axis=0)
                     for e in range(d, min(d + 2, LAGS))
                 ]
                 at = slice(d * TOK, (d + len(parts)) * TOK)

time: 37.2 us -> 37.1 us (level)
  no operation moved by 1% of the time
where the time goes in v6:
time: 37.1 us; the launch traced here: 37 us
  Pallas kernels  36.3 us (98%)
  between operations  0.64 us (2%)
    pallas_call x1, Pallas kernels, per_device(): pl.pallas_call(kernel, out_shape=(jax.ShapeDtypeStruct(rows, BF16), jax.S...  35.5 us
    pallas_call x1, Pallas kernels, per_device(): pl.pallas_call(finish, out_shape=(jax.ShapeDtypeStruct(rows, BF16), jax.S...  0.82 us

profile of v6, /device:TPU:1, one launch (start us, length us, event | category | flops | bytes accessed | tf_op | source)
XLA Modules:
  0.0 37.0 jit_solution(4704987938025714147)
XLA Ops:
  0.6 35.5 %shard_map.112 = (bf16[128,1024]{1,0:T(8,128)(2,1)S(1)}, bf16[128,1024]{1,0:T(8,128)(2,1)S(1)}, f32[32,2,128]{2,1,0:T(2,128)S(1)}) custom-call(s32[4]{0:T(128)} %doc_in.1, bf16[128,1024]{1,0:T(8,128)(2,1)} %go.1, bf16[128,1024]{1,0:T(8,128)(2,1)} %q.1, bf16[128,1024]{1,0:T(8,128)(2,1)} %k.1, bf16[128,1024]{1,0:T(8,128)(2,1)} %v.1, bf16[1024,4096]{1,0:T(8,128)(2,1)} %w.1, ...), custom_call_target="tpu_custom_call" | custom-call | tf_op jit(solution)/shard_map/pallas_call | solution.py:303
  36.2 0.8 %shard_map.113 = (bf16[128,1024]{1,0:T(8,128)(2,1)}, bf16[128,1024]{1,0:T(8,128)(2,1)}, f32[64,128]{1,0:T(8,128)}) custom-call(bf16[128,1024]{1,0:T(8,128)(2,1)S(1)} %get-tuple-element.6.out_q, bf16[128,1024]{1,0:T(8,128)(2,1)S(1)} %get-tuple-element.7.out_k, f32[32,2,128]{2,1,0:T(2,128)S(1)} %get-tuple-element.8.fr), custom_call_target="tpu_custom_call" | custom-call | tf_op jit(solution)/shard_map/pallas_call | solution.py:349

commit v7 on v6

--- a/solution.py
+++ b/solution.py
@@ -33,7 +33,7 @@
 def kernel(
     doc_in, go, q, k, v, w, filt, grp_in, skip_in,
     out_q, out_k, fr,
-    yr, perm, conv, qv, kv, skip, own, gov, vv, wv, fv, grp, doc, fg, rem, gs, gr, xs, xr, ys, toep, amat, gt, corr, fs, gain,
+    yr, perm, conv, qv, kv, skip, own, gov, vv, wv, fv, grp, doc, fg, gs, gr, xs, xr, ys, toep, amat, gt, corr, fs, gain,
     loc, ag_send, ag_recv, ex_send, ex_recv,
 ):
     i = lax.axis_index("ctx")
@@ -149,12 +149,9 @@
         on_down[n].start()
 
     l_doc.wait()
-    block = lax.shift_right_logical(iota((ROWS, TOK), 0), 4)
     ends = [doc[0]]
     for n in range(1, 4):
         ends.append(ends[-1] + doc[n])
-    end = jnp.where(block < ends[0], ends[0], jnp.where(block < ends[1], ends[1], jnp.where(block < ends[2], ends[2], ends[3])))
-    rem[...] = (end - block).astype(F32).astype(BF16).reshape(SPANS, PER, TOK)
     xr[:, SPANS:] = jnp.zeros((OWN, LAGS - 1, PER, TOK), BF16)
     corr[:, KW:] = jnp.zeros((TOK, TOK), F32)
 
@@ -324,7 +321,6 @@
             pltpu.VMEM((CH // TOK, TOK), jnp.int32),
             pltpu.SMEM((4,), jnp.int32),
             pltpu.VMEM(rows, F32),
-            pltpu.VMEM((SPANS, PER, TOK), BF16),
             pltpu.VMEM(blocks, BF16),
             pltpu.VMEM(blocks, BF16),
             pltpu.VMEM(blocks, BF16),

time: 37.1 us -> 37.1 us (level)
  no operation moved by 1% of the time
where the time goes in v7:
time: 37.1 us; the launch traced here: 37 us
  Pallas kernels  36.3 us (98%)
  between operations  0.64 us (2%)
    pallas_call x1, Pallas kernels, per_device(): pl.pallas_call(kernel, out_shape=(jax.ShapeDtypeStruct(rows, BF16), jax.S...  35.5 us
    pallas_call x1, Pallas kernels, per_device(): pl.pallas_call(finish, out_shape=(jax.ShapeDtypeStruct(rows, BF16), jax.S...  0.82 us

profile of v7, /device:TPU:1, one launch (start us, length us, event | category | flops | bytes accessed | tf_op | source)
XLA Modules:
  0.0 37.0 jit_solution(4704987938025714147)
XLA Ops:
  0.6 35.5 %shard_map.112 = (bf16[128,1024]{1,0:T(8,128)(2,1)S(1)}, bf16[128,1024]{1,0:T(8,128)(2,1)S(1)}, f32[32,2,128]{2,1,0:T(2,128)S(1)}) custom-call(s32[4]{0:T(128)} %doc_in.1, bf16[128,1024]{1,0:T(8,128)(2,1)} %go.1, bf16[128,1024]{1,0:T(8,128)(2,1)} %q.1, bf16[128,1024]{1,0:T(8,128)(2,1)} %k.1, bf16[128,1024]{1,0:T(8,128)(2,1)} %v.1, bf16[1024,4096]{1,0:T(8,128)(2,1)} %w.1, ...), custom_call_target="tpu_custom_call" | custom-call | tf_op jit(solution)/shard_map/pallas_call | solution.py:300
  36.2 0.8 %shard_map.113 = (bf16[128,1024]{1,0:T(8,128)(2,1)}, bf16[128,1024]{1,0:T(8,128)(2,1)}, f32[64,128]{1,0:T(8,128)}) custom-call(bf16[128,1024]{1,0:T(8,128)(2,1)S(1)} %get-tuple-element.6.out_q, bf16[128,1024]{1,0:T(8,128)(2,1)S(1)} %get-tuple-element.7.out_k, f32[32,2,128]{2,1,0:T(2,128)S(1)} %get-tuple-element.8.fr), custom_call_target="tpu_custom_call" | custom-call | tf_op jit(solution)/shard_map/pallas_call | solution.py:345
